TPU v7x, 128 devices: a whole 4x4x4 slice. The times are simulated.
128 devices in a mesh: fsdp: 32 (over x, y_lo, z), tensor: 4 (over y_hi, core).
Axes of the slice: x: 4, y: 4 (y_hi: 2, y_lo: 2; y = y_hi * 2 + y_lo), z: 4, core: 2. Of those that a mesh axis runs over, the one named last changes fastest.
Arguments:
- tokens: bfloat16 [24576, 5120], P('fsdp', 'tensor'), may hold values from -48 to 48
- live_rows: int32 [32], P('fsdp'), may hold values from 128 to 768, as said below
- first_row: int32 [24576], P('fsdp'), may hold values from 0 to 767, as said below
- w_query: bfloat16 [5120, 2560], P('fsdp', 'tensor'), may hold values from -1 to 1
- w_key: bfloat16 [5120, 512], P('fsdp', 'tensor'), may hold values from -1 to 1
- w_value: bfloat16 [5120, 512], P('fsdp', 'tensor'), may hold values from -0.078125 to 0.078125
- w_out: bfloat16 [2560, 5120], P('tensor', 'fsdp'), may hold values from -1 to 1
- query_gain: float32 [2560], P('tensor'), may hold values from 0.5 to 1.5
- key_gain: float32 [512], P('tensor'), may hold values from 0.5 to 1.5
- out_gain: float32 [5120], P('tensor'), may hold values from 0.5 to 1.5
Outputs:
- output: bfloat16 [24576, 5120], P('fsdp', 'tensor')
Inputs may be any that keep to these rules, and one draw needn't show every extreme that they name: `live_rows`: each entry is a multiple of 128; the largest value is reached on some index of every draw. `first_row`: each row's value is never above its own local index and never below the first local index of its pack (384 rows); the last row of each block begins a document of one row.
All inputs are finite; a program needn't handle non-finite values.
Results may differ from a plain program's by a relative error of at most 0.009.
Values may be sent and summed in bfloat16 or wider, within the bound.
A program may use at most 128 MiB of HBM per device.

v0:
```python
import math

import jax
import jax.numpy as jnp
from jax import lax
from jax.sharding import PartitionSpec as P

D = 5120
HEADS = 20
KV_HEADS = 4
HEAD_DIM = 128
BLOCK = 128


EPS = 1e-06
ROPE_BASE = 500000.0


def rotate(field, positions):
    half_dim = field.shape[-1] // 2
    freqs = jnp.power(ROPE_BASE, -(jnp.arange(half_dim, dtype=jnp.float32) * 2.0 / field.shape[-1]))
    angle = positions[:, None] * freqs[None, :]
    cosine = jnp.cos(angle)[:, None, :]
    sine_part = jnp.sin(angle)[:, None, :]
    first = field[..., :half_dim]
    second = field[..., half_dim:]
    return jnp.concatenate(
        [first * cosine - second * sine_part, second * cosine + first * sine_part], axis=-1
    )


def attend(queries, keys, values, starts, offset):
    row_count = queries.shape[0]
    kv_count = keys.shape[1]
    group_size = queries.shape[1] // kv_count
    grouped = queries.reshape(row_count, kv_count, group_size, HEAD_DIM)
    scores = jnp.einsum(
        "qkgd,skd->kgqs", grouped, keys, preferred_element_type=jnp.float32
    ) / math.sqrt(HEAD_DIM)
    local = jnp.arange(row_count, dtype=jnp.int32)
    allowed = (local[None, :] >= (starts - offset)[:, None]) & (local[None, :] <= local[:, None])
    scores = jnp.where(allowed[None, None], scores, jnp.float32(-1e30))
    peak_value = jnp.max(scores, axis=-1, keepdims=True)
    expo = jnp.exp(scores - peak_value)
    totals = jnp.sum(expo, axis=-1, keepdims=True)
    probs = (expo / totals).astype(jnp.bfloat16)
    mixed = jnp.einsum("kgqs,skd->qkgd", probs, values, preferred_element_type=jnp.float32)
    return mixed.reshape(row_count, -1).astype(jnp.bfloat16)


def project(features, matrices, counts, half_rows):
    capacity = features.shape[0]
    results = tuple((jnp.zeros((capacity, matrix.shape[1]), jnp.float32) for matrix in matrices))
    for pack_index in range(2):

        def block_step(number, carried, pack_index=pack_index):
            row_start = pack_index * half_rows + number * BLOCK
            piece = lax.dynamic_slice_in_dim(features, row_start, BLOCK, 0)
            return tuple(
                (
                    lax.dynamic_update_slice_in_dim(
                        current,
                        jnp.dot(piece, matrix, preferred_element_type=jnp.float32),
                        row_start,
                        0,
                    )
                    for current, matrix in zip(carried, matrices)
                )
            )

        results = lax.fori_loop(0, counts[pack_index] // BLOCK, block_step, results)
    return results


def layer_rows(
    local_tokens, counts, starts, w_query, w_key, w_value, w_out, query_gain, key_gain, out_gain
):
    capacity = local_tokens.shape[0]
    half_rows = capacity // 2
    features = lax.all_gather(local_tokens, "tensor", axis=1, tiled=True)
    full_query, full_key, full_value = (
        lax.all_gather(w_query, "fsdp", axis=0, tiled=True),
        lax.all_gather(w_key, "fsdp", axis=0, tiled=True),
        lax.all_gather(w_value, "fsdp", axis=0, tiled=True),
    )
    query, key, value = project(features, (full_query, full_key, full_value), counts, half_rows)
    query_sq, key_sq = lax.psum(
        (jnp.sum(query * query, axis=1), jnp.sum(key * key, axis=1)), "tensor"
    )
    query_normed = query * lax.rsqrt(query_sq / (HEADS * HEAD_DIM) + EPS)[:, None] * query_gain
    key_normed = key * lax.rsqrt(key_sq / (KV_HEADS * HEAD_DIM) + EPS)[:, None] * key_gain
    row_ids = jnp.arange(capacity, dtype=jnp.int32)
    positions = (row_ids - starts).astype(jnp.float32)
    query_rot = rotate(query_normed.reshape(capacity, -1, HEAD_DIM), positions).astype(jnp.bfloat16)
    key_rot = rotate(key_normed.reshape(capacity, -1, HEAD_DIM), positions).astype(jnp.bfloat16)
    value_heads = value.astype(jnp.bfloat16).reshape(capacity, -1, HEAD_DIM)
    packs = []
    for pack_index in range(2):
        lower = pack_index * half_rows
        packs.append(
            attend(
                query_rot[lower : lower + half_rows],
                key_rot[lower : lower + half_rows],
                value_heads[lower : lower + half_rows],
                starts[lower : lower + half_rows],
                lower,
            )
        )
    attended = jnp.concatenate(packs, axis=0)
    full_out = lax.all_gather(w_out, "fsdp", axis=1, tiled=True)
    (partial_value,) = project(attended, (full_out,), counts, half_rows)
    attn_out = lax.psum_scatter(
        partial_value.astype(jnp.bfloat16), "tensor", scatter_dimension=1, tiled=True
    ).astype(jnp.float32)
    out_sq = lax.psum(jnp.sum(attn_out * attn_out, axis=1), "tensor")
    scale = lax.rsqrt(out_sq / D + EPS)[:, None]
    result = (local_tokens.astype(jnp.float32) + attn_out * scale * out_gain).astype(jnp.bfloat16)
    limit = jnp.where(row_ids < half_rows, counts[0], half_rows + counts[1])
    return jnp.where((row_ids < limit)[:, None], result, jnp.zeros_like(result))


def body(
    tokens, live_rows, first_row, w_query, w_key, w_value, w_out, query_gain, key_gain, out_gain
):
    capacity = tokens.shape[0]
    half_rows = capacity // 2
    live_count = live_rows[0]
    count_low = jnp.minimum(live_count, half_rows)
    count_high = jnp.maximum(live_count - half_rows, 0)
    return layer_rows(
        tokens,
        (count_low, count_high),
        first_row,
        w_query,
        w_key,
        w_value,
        w_out,
        query_gain,
        key_gain,
        out_gain,
    )


def solution(mesh):
    in_specs = (
        P("fsdp", "tensor"),
        P("fsdp"),
        P("fsdp"),
        P("fsdp", "tensor"),
        P("fsdp", "tensor"),
        P("fsdp", "tensor"),
        P("tensor", "fsdp"),
        P("tensor"),
        P("tensor"),
        P("tensor"),
    )
    out_specs = P("fsdp", "tensor")
    return jax.shard_map(body, mesh=mesh, in_specs=in_specs, out_specs=out_specs, check_vma=False)
```

profile of v0, /device:TPU:1, one launch (start us, length us, event | category | flops | bytes accessed | tf_op | source)
XLA Modules:
  0.0 840.2 jit_solution(14680716694172130130)
XLA Ops:
  14.5 126.5 %all-gather.10.cloned.1.call-done = bf16[5120,128]{1,0:T(8,128)(2,1)} async-done(((bf16[160,128]{1,0:T(8,128)(2,1)}), bf16[5120,128]{1,0:T(8,128)(2,1)}) %all-gather.10.cloned.1.call-update) | async-done | bytes 1310736 | tf_op jit(solution)/shard_map/all_gather | solution.py:83
  141.0 153.0 %all-gather.12.cloned.1.call-done = bf16[5120,128]{1,0:T(8,128)(2,1)} async-done(((bf16[160,128]{1,0:T(8,128)(2,1)}), bf16[5120,128]{1,0:T(8,128)(2,1)}) %all-gather.12.cloned.1.call-update) | async-done | bytes 1310736 | tf_op jit(solution)/shard_map/all_gather | solution.py:84
  293.9 84.0 %all-gather.6.cloned.1.call-done = bf16[768,5120]{1,0:T(8,128)(2,1)} async-done(((bf16[768,1280]{1,0:T(8,128)(2,1)}), bf16[768,5120]{1,0:T(8,128)(2,1)}) %all-gather.6.cloned.1.call-update) | async-done | bytes 7864336 | tf_op jit(solution)/shard_map/all_gather | solution.py:80
  377.9 142.6 %all-gather.8.cloned.1.call-done = bf16[5120,640]{1,0:T(8,128)(2,1)} async-done(((bf16[160,640]{1,0:T(8,128)(2,1)}), bf16[5120,640]{1,0:T(8,128)(2,1)}) %all-gather.8.cloned.1.call-update) | async-done | bytes 6553616 | tf_op jit(solution)/shard_map/all_gather | solution.py:82
  520.6 25.2 %while.52 = (s32[]{:T(128)}, f32[768,640]{1,0:T(8,128)S(1)}, f32[768,128]{1,0:T(8,128)S(1)}, bf16[768,128]{1,0:T(8,128)(2,1)S(1)}, s32[]{:T(128)}, /*index=5*/bf...) while((s32[]{:T(128)}, f32[768,640]{1,0:T(8,128)S(1)}, ...), condition=%wide.region_1.2_spmd, body=%wide.region_0.1_spmd.sunk | while | flops 1174405120 | bytes 24055012 | solution.py:71
  520.7 4.6 convolution_dynamic-update-slice_fusion.16
  537.5 4.6 convolution_dynamic-update-slice_fusion.16
  545.8 25.3 %while.53 = (s32[]{:T(128)}, f32[768,640]{1,0:T(8,128)S(1)}, f32[768,128]{1,0:T(8,128)S(1)}, bf16[768,128]{1,0:T(8,128)(2,1)S(1)}, s32[]{:T(128)}, /*index=5*/bf...) while((s32[]{:T(128)}, f32[768,640]{1,0:T(8,128)S(1)}, ...), condition=%wide.region_3.4_spmd, body=%wide.region_2.3_spmd.sunk | while | flops 1174405120 | bytes 24055032 | solution.py:71
  545.9 4.6 convolution_dynamic-update-slice_fusion.19
  554.3 4.6 convolution_dynamic-update-slice_fusion.19
  562.8 4.6 convolution_dynamic-update-slice_fusion.19
  574.2 28.0 %all-reduce = (f32[768]{0:T(1024)S(1)}, f32[768]{0:T(1024)S(1)}) all-reduce(f32[768]{0:T(1024)S(1)} %multiply_reduce_fusion, f32[768]{0:T(1024)S(1)} %multiply_reduce_fusion.1), channel_id=1, replica_groups=mesh['fsdp'=32,'tensor'=4] {'tensor'}, use_global_device_ids=true, to_apply=%region_7.8 | all-reduce | flops 1536 | bytes 12288 | tf_op jit(solution)/shard_map/psum | solution.py:87
  617.6 67.1 %all-gather.14.cloned.1.call-done = bf16[640,5120]{0,1:T(8,128)(2,1)} async-done(((bf16[640,160]{0,1:T(8,128)(2,1)}), bf16[640,5120]{0,1:T(8,128)(2,1)}) %all-gather.14.cloned.1.call-update) | async-done | bytes 6553616 | tf_op jit(solution)/shard_map/all_gather | solution.py:110
  684.7 9.5 %copy.47 = bf16[640,5120]{1,0:T(8,128)(2,1)} copy(bf16[640,5120]{0,1:T(8,128)(2,1)} %all-gather.14.cloned.1.call-done) | data formatting | bytes 13107200 | tf_op jit(solution)/shard_map/while | solution.py:71
  698.3 15.4 %while.54 = (s32[]{:T(128)}, bf16[768,5120]{1,0:T(8,128)(2,1)}, s32[]{:T(128)}, bf16[768,640]{1,0:T(8,128)(2,1)S(1)}, bf16[640,5120]{1,0:T(8,128)(2,1)}, /*index=5*/s32[]{:T(128)}, s32[]{:T(128)}, s32[]{:T(128)}, s32[]{:T(128)}) while((s32[]{:T(128)}, bf16[768,5120]{1,0:T(8,128)(2,1)}, s32[]{:T(128)}, bf16[768,640]{1,0:T(8,128)(2,1)S(1)}, ...), condition=%wide.region_13.14_spmd, body=%wide.region_12.13_spmd.sunk | while | flops 838860800 | bytes 9340043 | solution.py:71
  698.3 5.1 convolution_dynamic-update-slice_fusion.22
  703.4 5.1 convolution_dynamic-update-slice_fusion.22
  708.5 5.1 convolution_dynamic-update-slice_fusion.22
  713.6 15.4 %while.55 = (s32[]{:T(128)}, bf16[768,5120]{1,0:T(8,128)(2,1)}, s32[]{:T(128)}, bf16[768,640]{1,0:T(8,128)(2,1)S(1)}, bf16[640,5120]{1,0:T(8,128)(2,1)}, /*index...) while((s32[]{:T(128)}, bf16[768,5120]{1,0:T(8,128)(2,1)}, s32[]{:T(128)}, ...), condition=%wide.region_15.16_spmd, body=%wide.region_14.15_spmd.sunk | while | flops 838860800 | bytes 9340063 | solution.py:71
  713.6 5.1 convolution_dynamic-update-slice_fusion.23
  718.8 5.2 convolution_dynamic-update-slice_fusion.23
  723.9 5.1 convolution_dynamic-update-slice_fusion.23
  729.1 91.1 %reduce-scatter.2.cloned.1.call-done = bf16[768,1280]{1,0:T(8,128)(2,1)} async-done(((bf16[768,5120]{1,0:T(8,128)(2,1)}), bf16[768,1280]{1,0:T(8,128)(2,1)}) %reduce-scatter.2.cloned.1.call-update) | async-done | bytes 1966096 | tf_op jit(solution)/shard_map/reduce_scatter | solution.py:112
  822.2 7.4 psum.23
  (104 shorter events, 62.7 us)
Async XLA Ops:
  6.5 134.5 %all-gather.10.cloned.1.call-start = ((), (), s32[]{:S(2)}) async-start(), calls=%async_computation.3 | async-start | bytes 1351680 | tf_op jit(solution)/shard_map/all_gather | solution.py:83
  7.3 286.7 %all-gather.12.cloned.1.call-start = ((), (), s32[]{:S(2)}) async-start(), calls=%async_computation.4 | async-start | bytes 1351680 | tf_op jit(solution)/shard_map/all_gather | solution.py:84
  8.0 369.9 %all-gather.6.cloned.1.call-start = ((), (), s32[]{:S(2)}) async-start(), calls=%async_computation.1 | async-start | bytes 9830400 | tf_op jit(solution)/shard_map/all_gather | solution.py:80
  8.7 511.7 %all-gather.8.cloned.1.call-start = ((), (), s32[]{:S(2)}) async-start(), calls=%async_computation.2 | async-start | bytes 6758400 | tf_op jit(solution)/shard_map/all_gather | solution.py:82
  9.3 675.4 %all-gather.14.cloned.1.call-start = ((), (), s32[]{:S(2)}) async-start(), calls=%async_computation.5 | async-start | bytes 6758400 | tf_op jit(solution)/shard_map/all_gather | solution.py:110
  9.9 810.3 %reduce-scatter.2.cloned.1.call-start = ((), (), s32[]{:S(2)}) async-start(), calls=%async_computation.6 | async-start | bytes 9830400 | tf_op jit(solution)/shard_map/reduce_scatter | solution.py:112
  520.7 4.6 copy-start
  525.2 2.0 copy-start.2
  529.1 4.6 copy-start
  533.6 2.0 copy-start.2
  537.4 4.6 copy-start
  545.9 4.6 copy-start.1
  550.4 2.0 copy-start.3
  554.3 4.6 copy-start.1
  558.9 2.0 copy-start.3
  562.8 4.6 copy-start.1
  567.3 2.0 copy-start.3
  572.0 30.2 %copy-start.12 = (f32[640]{0:T(1024)S(1)}, f32[640]{0:T(1024)}, u32[]{:S(2)}) copy-start(f32[640]{0:T(1024)} %param.25) | copy-start | bytes 7684
  604.1 3.8 copy-start.8
  604.1 3.9 copy-start.13
  608.0 5.2 copy-start.9
  609.0 2.7 copy-start.6
  729.0 100.6 %copy-start.11 = (f32[1280]{0:T(1024)S(1)}, f32[1280]{0:T(1024)}, u32[]{:S(2)}) copy-start(f32[1280]{0:T(1024)} %param.27) | copy-start | bytes 15364
  729.1 100.6 %copy-start.4 = (bf16[768,1280]{1,0:T(8,128)(2,1)S(1)}, bf16[768,1280]{1,0:T(8,128)(2,1)}, u32[]{:S(2)}) copy-start(bf16[768,1280]{1,0:T(8,128)(2,1)} %param.18) | copy-start | bytes 5898244
  (4 other events, 5.5 us)
Sparse Core Ops, SparseCore 0:
  9.0 131.9 all-gather.9
  142.6 151.2 all-gather.11
  295.6 82.2 all-gather.5
  379.4 141.0 all-gather.7
  522.0 162.7 all-gather.13
  729.2 91.0 reduce-scatter.1
where the time goes:
time: 841 us; the launch traced here: 840 us
  waiting for transfers between devices  667 us (79%)
  matrix products  84.7 us (10%)
  blocking collectives  35.3 us (4%)
  local copies, waits for them, and re-layouts  21 us (2%)
  other arithmetic  16.7 us (2%)
  between operations  14.4 us (2%)
    all_gather x1, waiting for transfers between devices, layer_rows(): lax.all_gather(w_value, 'fsdp', axis=0, tiled=True)  153 us
    all_gather x1, waiting for transfers between devices, layer_rows(): lax.all_gather(w_query, 'fsdp', axis=0, tiled=True)  143 us
    all_gather x1, waiting for transfers between devices, layer_rows(): lax.all_gather(w_key, 'fsdp', axis=0, tiled=True)  127 us
    reduce_scatter x1, waiting for transfers between devices, layer_rows(): lax.psum_scatter(partial_value.astype(jnp.bfloat16), 'tensor', scatter_di...  91.1 us
    all_gather x1, waiting for transfers between devices, layer_rows(): features = lax.all_gather(local_tokens, 'tensor', axis=1, tiled=True)  84 us
    dot_general x24, matrix products, block_step(): jnp.dot(piece, matrix, preferred_element_type=jnp.float32)  80.8 us
    all_gather x1, waiting for transfers between devices, layer_rows(): full_out = lax.all_gather(w_out, 'fsdp', axis=1, tiled=True)  67.1 us
    psum x1, blocking collectives, layer_rows(): lax.psum((jnp.sum(query * query, axis=1), jnp.sum(key * key, axis=1)), 't...  28 us
  transfers between devices with their start and end apart: 6, of which 6 were waited for; matrix products, arithmetic and copies ran while one was open for 9% of the time, Pallas kernels for 0%

commit v1 on v0

v1 whole, which is shorter than its diff:
```python
import functools
import math

import jax
import jax.numpy as jnp
from jax import lax
from jax.experimental import pallas as pl
from jax.experimental.pallas import tpu as pltpu
from jax.sharding import PartitionSpec as P

D = 5120
HEADS = 20
KV_HEADS = 4
HEAD_DIM = 128
CAP = 768
HALF = 384
EPS = 1e-06
ROPE_BASE = 500000.0
SHARD = 160
QKV = 896
QW = 640
TCOL = 1280
MESH = pl.DeviceIdType.MESH

TOK_CHUNK = 64
TOK_N = CAP // TOK_CHUNK
ATT_CHUNK = 128
ATT_N = CAP // ATT_CHUNK

AG_SEMS = 1 + 2 * 22
SEM_W = 0
SEM_O = SEM_W + AG_SEMS
SEM_T = SEM_O + AG_SEMS
SEM_A = SEM_T + 4 * TOK_N
SEM_S = SEM_A + 4 * ATT_N
SEM_P = SEM_S + 6
SEM_N = SEM_P + 1


def kernel(
    tok_hbm,
    wq_hbm,
    wk_hbm,
    wv_hbm,
    wot_hbm,
    cos_ref,
    sin_ref,
    start_ref,
    gain_ref,
    ogain_ref,
    live_ref,
    out_hbm,
    wbuf,
    obuf,
    xall,
    xstage,
    acc,
    rot,
    vbuf,
    att,
    astage,
    oacc,
    res,
    sqt,
    sqr,
    send_sem,
    recv_sem,
    local_sem,
):
    f = lax.axis_index("fsdp")
    t = lax.axis_index("tensor")
    x, yl, z = f // 8, (f // 4) % 2, f % 4
    yh, core = t // 2, t % 2
    y = 2 * yh + yl

    def dev(dx=0, dy=0, dz=0, flip=0):
        ny = (y + dy) % 4
        nf = ((x + dx) % 4) * 8 + (ny % 2) * 4 + (z + dz) % 4
        nc = (core + flip) % 2
        return (nf, (ny // 2) * 2 + nc)

    ypair = ((x * 8 + (1 - yl) * 4 + z), t)
    swap_f = t * 8 + yl * 4 + z
    swap = (swap_f, x)
    sends = []

    def send(src, dst, idx, to):
        copy = pltpu.make_async_remote_copy(
            src_ref=src,
            dst_ref=dst,
            send_sem=send_sem.at[idx],
            recv_sem=recv_sem.at[idx],
            device_id=to,
            device_id_type=MESH,
        )
        copy.start()
        sends.append(copy)

    def recv(dst, idx):
        pltpu.make_async_remote_copy(
            src_ref=dst,
            dst_ref=dst,
            send_sem=send_sem.at[idx],
            recv_sem=recv_sem.at[idx],
            device_id=ypair,
            device_id_type=MESH,
        ).wait_recv()

    events = []

    def at(time, fn):
        events.append((time, len(events), fn))

    local = [
        pltpu.make_async_copy(wq_hbm, wbuf.at[x, yl, z, :, pl.ds(0, QW)], local_sem.at[0]),
        pltpu.make_async_copy(wk_hbm, wbuf.at[x, yl, z, :, pl.ds(QW, 128)], local_sem.at[1]),
        pltpu.make_async_copy(wv_hbm, wbuf.at[x, yl, z, :, pl.ds(QW + 128, 128)], local_sem.at[2]),
        pltpu.make_async_copy(tok_hbm, xall.at[t], local_sem.at[3]),
    ]
    for copy in local:
        copy.start()

    barrier = pltpu.get_barrier_semaphore()
    partners = [
        dev(dx=1), dev(dx=3), dev(dz=1), dev(dz=3), dev(dy=1), dev(dy=3),
        dev(flip=1), dev(dy=2), dev(dy=2, flip=1),
    ]
    for to in partners:
        pl.semaphore_signal(barrier, inc=1, device_id=to, device_id_type=MESH)

    @pl.when(x != t)
    def _():
        pl.semaphore_signal(barrier, inc=1, device_id=swap, device_id_type=MESH)

    pl.semaphore_wait(barrier, len(partners) + jnp.where(x != t, 1, 0))

    def gather(buf, base, times):
        def slot(color, da, yy, db):
            dx, dz = (da, db) if color == 0 else (db, da)
            rows = pl.ds(color * 80, 80)
            return buf.at[(x + dx) % 4, yy, (z + dz) % 4, rows]

        def pair(color, da, db):
            dx, dz = (da, db) if color == 0 else (db, da)
            rows = pl.ds(color * 80, 80)
            return buf.at[(x + dx) % 4, :, (z + dz) % 4, rows]

        def step(color, stage, sign):
            d = sign % 4
            along_x = (stage == 0) == (color == 0)
            return dev(dx=d) if along_x else dev(dz=d)

        def sem(color, k):
            return base + 1 + color * 22 + k

        def e0():
            own = buf.at[x, yl, z]
            send(own, own, base, ypair)
            for c in range(2):
                send(slot(c, 0, yl, 0), slot(c, 0, yl, 0), sem(c, 0), step(c, 0, 1))
                send(slot(c, 0, yl, 0), slot(c, 0, yl, 0), sem(c, 1), step(c, 0, -1))

        def second(c, da, k):
            send(pair(c, da, 0), pair(c, da, 0), sem(c, 6 + 4 * k), step(c, 1, 1))
            send(pair(c, da, 0), pair(c, da, 0), sem(c, 7 + 4 * k), step(c, 1, -1))

        def e1():
            recv(buf.at[x, 1 - yl, z], base)
            for c in range(2):
                send(slot(c, 0, 1 - yl, 0), slot(c, 0, 1 - yl, 0), sem(c, 2), step(c, 0, 1))
                send(slot(c, 0, 1 - yl, 0), slot(c, 0, 1 - yl, 0), sem(c, 3), step(c, 0, -1))
            for c in range(2):
                second(c, 0, 0)

        def e2():
            for c in range(2):
                recv(slot(c, 3, yl, 0), sem(c, 0))
                recv(slot(c, 1, yl, 0), sem(c, 1))
                recv(slot(c, 3, 1 - yl, 0), sem(c, 2))
                recv(slot(c, 1, 1 - yl, 0), sem(c, 3))
                send(slot(c, 3, 0, 0), slot(c, 3, 0, 0), sem(c, 4), step(c, 0, 1))
                send(slot(c, 1, 1, 0), slot(c, 1, 1, 0), sem(c, 5), step(c, 0, -1))
            for c in range(2):
                second(c, 3, 1)
            for c in range(2):
                second(c, 1, 2)

        def e3():
            for c in range(2):
                recv(slot(c, 2, 0, 0), sem(c, 4))
                recv(slot(c, 2, 1, 0), sem(c, 5))
                second(c, 2, 3)

        order = (0, 3, 1, 2)

        def e4(k):
            da = order[k]
            for c in range(2):
                recv(pair(c, da, 3), sem(c, 6 + 4 * k))
                recv(pair(c, da, 1), sem(c, 7 + 4 * k))
                send(slot(c, da, 0, 3), slot(c, da, 0, 3), sem(c, 8 + 4 * k), step(c, 1, 1))
                send(slot(c, da, 1, 1), slot(c, da, 1, 1), sem(c, 9 + 4 * k), step(c, 1, -1))

        def e5(k):
            da = order[k]
            for c in range(2):
                recv(slot(c, da, 0, 2), sem(c, 8 + 4 * k))
                recv(slot(c, da, 1, 2), sem(c, 9 + 4 * k))

        fns = (
            e0, e1, e2, e3,
            lambda: e4(0), lambda: e4(1), lambda: e4(2), lambda: e4(3),
            lambda: e5(0), lambda: e5(1), lambda: e5(2), lambda: e5(3),
        )
        for when, fn in zip(times, fns):
            at(when, fn)

    def origin_hi(dy):
        return ((y + dy) % 4) // 2

    def rows_out(buf, stage, base, n, chunk, i, src=None):
        rows = pl.ds(i * chunk, chunk)
        srows = pl.ds((i // 2) * chunk, chunk)
        own = buf.at[t, rows] if src is None else src.at[rows]
        d = 1 if i % 2 == 0 else 3
        send(own, stage.at[i % 2, srows], base + 4 * i, dev(dy=d))
        send(own, buf.at[t, rows], base + 4 * i + 1, dev(flip=1))

    def rows_relay(buf, stage, base, n, chunk, i):
        rows = pl.ds(i * chunk, chunk)
        srows = pl.ds((i // 2) * chunk, chunk)
        d = 1 if i % 2 == 0 else 3
        recv(stage.at[i % 2, srows], base + 4 * i)
        came = origin_hi(4 - d) * 2 + core
        send(stage.at[i % 2, srows], buf.at[came, rows], base + 4 * i + 2, dev(dy=d))

    def rows_in(buf, stage, base, n, chunk, i):
        rows = pl.ds(i * chunk, chunk)
        far = (t + 2) % 4
        recv(buf.at[far, rows], base + 4 * i + 2)
        send(buf.at[far, rows], buf.at[far, rows], base + 4 * i + 3, dev(flip=1))

    def rows_done(buf, stage, base, n, chunk, i):
        rows = pl.ds(i * chunk, chunk)
        sib = (core + 1) % 2
        recv(buf.at[yh * 2 + sib, rows], base + 4 * i + 1)
        recv(buf.at[(1 - yh) * 2 + sib, rows], base + 4 * i + 3)

    tok = (xall, xstage, SEM_T, TOK_N, TOK_CHUNK)
    atd = (att, astage, SEM_A, ATT_N, ATT_CHUNK)

    def exchange(k):
        for n, to in enumerate((dev(flip=1), dev(dy=2), dev(dy=2, flip=1))):
            send(sqt.at[k, pl.ds(0, 8)], sqr.at[k, n], SEM_S + 3 * k + n, to)

    def exchanged(k):
        total = sqt[k, pl.ds(0, 8)]
        for n in range(3):
            recv(sqr.at[k, n], SEM_S + 3 * k + n)
            total = total + sqr[k, n]
        return jnp.concatenate([total] * 16, axis=0).T

    def qkv(p, dx, first):
        j = (x + dx) % 4
        rows = pl.ds(p * HALF, HALF)
        part = jnp.dot(
            xall[j, rows], wbuf[j].reshape(TCOL, QKV), preferred_element_type=jnp.float32
        )
        if first:
            acc[rows] = part
        else:
            acc[rows] += part

    lane = lax.broadcasted_iota(jnp.int32, (HALF, 128), 1)

    def sums(p):
        rows = pl.ds(p * HALF, HALF)
        q = acc[rows, pl.ds(0, QW)]
        k = acc[rows, pl.ds(QW, 128)]
        qs = jnp.sum(q * q, axis=1, keepdims=True)
        ks = jnp.sum(k * k, axis=1, keepdims=True)
        both = jnp.where(lane < 4, qs, ks)
        sqt[0, :, rows] = both.T

    def rotate():
        total = exchanged(0)
        res_q = lax.rsqrt(total[:, 0:1] / (HEADS * HEAD_DIM) + EPS)
        res_k = lax.rsqrt(total[:, 4:5] / (KV_HEADS * HEAD_DIM) + EPS)
        for h in range(6):
            cols = pl.ds(h * 128, 128)
            u = acc[:, cols] * (res_q if h < 5 else res_k) * gain_ref[:, cols]
            r = u * cos_ref[...] + pltpu.roll(u, 64, 1) * sin_ref[...]
            rot[:, cols] = r.astype(jnp.bfloat16)
        vbuf[...] = acc[:, pl.ds(QW + 128, 128)].astype(jnp.bfloat16)

    def attend(p, b):
        rows = pl.ds(p * HALF + b * 128, 128)
        width = (b + 1) * 128
        seen = pl.ds(p * HALF, width)
        kk = rot[seen, pl.ds(QW, 128)]
        vv = vbuf[seen]
        first = start_ref[rows] - p * HALF
        col = lax.broadcasted_iota(jnp.int32, (128, width), 1)
        row = lax.broadcasted_iota(jnp.int32, (128, width), 0) + b * 128
        allowed = (col >= first) & (col <= row)
        for h in range(5):
            cols = pl.ds(h * 128, 128)
            s = lax.dot_general(
                rot[rows, cols], kk, (((1,), (1,)), ((), ())), preferred_element_type=jnp.float32
            )
            s = jnp.where(allowed, s * (1.0 / math.sqrt(HEAD_DIM)), jnp.float32(-1e30))
            e = jnp.exp(s - jnp.max(s, axis=1, keepdims=True))
            probs = (e * (1.0 / jnp.sum(e, axis=1, keepdims=True))).astype(jnp.bfloat16)
            o = jnp.dot(probs, vv, preferred_element_type=jnp.float32)
            att[t, rows, cols] = o.astype(jnp.bfloat16)

    def project(p, j, first):
        rows = pl.ds(p * HALF, HALF)
        part = lax.dot_general(
            att[j, rows],
            obuf[j].reshape(TCOL, QW),
            (((1,), (1,)), ((), ())),
            preferred_element_type=jnp.float32,
        )
        if first:
            oacc[rows] = part
        else:
            oacc[rows] += part

    def out_sums(p):
        rows = pl.ds(p * HALF, HALF)
        o = oacc[rows]
        sqt[1, :, rows] = jnp.broadcast_to(jnp.sum(o * o, axis=1, keepdims=True), (HALF, 128)).T

    def finish():
        total = exchanged(1)
        live = live_ref[0]
        for p in range(2):
            rows = pl.ds(p * HALF, HALF)
            scale = lax.rsqrt(total[p * HALF : (p + 1) * HALF, 0:1] / D + EPS)
            r = xall[t, rows].astype(jnp.float32) + oacc[rows] * scale * ogain_ref[...]
            row = lax.broadcasted_iota(jnp.int32, (HALF, TCOL), 0) + p * HALF
            res[rows] = jnp.where(row < live, r, 0.0).astype(jnp.bfloat16)
        done = pltpu.make_async_copy(res, out_hbm, local_sem.at[0])
        done.start()
        done.wait()

    for copy in local[:3]:
        copy.wait()
    gather(wbuf, SEM_W, (0, 8, 12, 20, 19, 26, 32, 38, 32.5, 40, 44, 50))

    own_o = obuf.at[x, yl, z]

    def swap_out():
        @pl.when(x != t)
        def _():
            copy = pltpu.make_async_remote_copy(
                src_ref=wot_hbm, dst_ref=obuf.at[t, yl, z], send_sem=send_sem.at[SEM_P],
                recv_sem=recv_sem.at[SEM_P], device_id=swap, device_id_type=MESH,
            )
            copy.start()

        @pl.when(x == t)
        def _():
            copy = pltpu.make_async_copy(wot_hbm, own_o, local_sem.at[4])
            copy.start()

    def swap_in():
        @pl.when(x != t)
        def _():
            copy = pltpu.make_async_remote_copy(
                src_ref=wot_hbm, dst_ref=own_o, send_sem=send_sem.at[SEM_P],
                recv_sem=recv_sem.at[SEM_P], device_id=swap, device_id_type=MESH,
            )
            copy.wait()

        @pl.when(x == t)
        def _():
            copy = pltpu.make_async_copy(wot_hbm, own_o, local_sem.at[4])
            copy.wait()

    at(1.5, swap_out)
    for i in range(TOK_N):
        at(1.0, functools.partial(rows_out, *tok, i, tok_hbm))
        at(10 + 7 * (i // 2), functools.partial(rows_relay, *tok, i))
        at(17 + 7 * (i // 2), functools.partial(rows_in, *tok, i))
    for i in range(TOK_N // 2):
        at(33, functools.partial(rows_done, *tok, i))
    at(33.1, lambda: local[3].wait())
    at(33.2, functools.partial(qkv, 0, 0, True))
    for i in range(TOK_N // 2, TOK_N):
        at(53, functools.partial(rows_done, *tok, i))
    at(53.1, functools.partial(qkv, 1, 0, True))
    for n, dx in enumerate((3, 1, 2)):
        for p in range(2):
            at(53.2 + n / 10, functools.partial(qkv, p, dx, False))

    at(39, swap_in)
    gather(obuf, SEM_O, (39.1, 46, 53.15, 58, 58, 61, 62.5, 64, 69, 70, 72, 82))

    at(54, lambda: sums(0))
    at(54, lambda: sums(1))
    at(54.1, lambda: exchange(0))
    at(60, rotate)
    for i in range(ATT_N):
        at(63 + 2.5 * i, functools.partial(attend, i // 3, i % 3))
        at(63.1 + 2.5 * i, functools.partial(rows_out, *atd, i))
        at(69 + 2.5 * i, functools.partial(rows_relay, *atd, i))
        at(75 + 2.5 * i, functools.partial(rows_in, *atd, i))
    for p in range(2):
        at(82.5, functools.partial(project, p, t, True))
    for i in range(ATT_N):
        at(88, functools.partial(rows_done, *atd, i))
    for n in range(1, 4):
        for p in range(2):
            at(89 + n / 10, functools.partial(project, p, (t + n) % 4, False))
    at(95, lambda: out_sums(0))
    at(95, lambda: out_sums(1))
    at(95.1, lambda: exchange(1))
    at(96, finish)

    for _, _, fn in sorted(events, key=lambda e: (e[0], e[1])):
        fn()
    for copy in sends:
        copy.wait_send()


def body(
    tokens, live_rows, first_row, w_query, w_key, w_value, w_out, query_gain, key_gain, out_gain
):
    half = HEAD_DIM // 2
    freqs = jnp.power(ROPE_BASE, -(jnp.arange(half, dtype=jnp.float32) * 2.0 / HEAD_DIM))
    positions = (jnp.arange(CAP, dtype=jnp.int32) - first_row).astype(jnp.float32)
    angle = positions[:, None] * freqs[None, :]
    cosine, sine = jnp.cos(angle), jnp.sin(angle)
    cos = jnp.concatenate([cosine, cosine], axis=1)
    sin = jnp.concatenate([-sine, sine], axis=1)
    gains = jnp.concatenate([query_gain, key_gain])[None, :]
    hbm = pl.BlockSpec(memory_space=pl.ANY)
    vmem = pl.BlockSpec(memory_space=pltpu.VMEM)
    smem = pl.BlockSpec(memory_space=pltpu.SMEM)
    bf, fl = jnp.bfloat16, jnp.float32
    return pl.pallas_call(
        kernel,
        out_shape=jax.ShapeDtypeStruct((CAP, TCOL), bf),
        in_specs=[hbm] * 5 + [vmem] * 5 + [smem],
        out_specs=hbm,
        scratch_shapes=[
            pltpu.VMEM((4, 2, 4, SHARD, QKV), bf),
            pltpu.VMEM((4, 2, 4, SHARD, QW), bf),
            pltpu.VMEM((4, CAP, TCOL), bf),
            pltpu.VMEM((2, HALF, TCOL), bf),
            pltpu.VMEM((CAP, QKV), fl),
            pltpu.VMEM((CAP, QW + 128), bf),
            pltpu.VMEM((CAP, 128), bf),
            pltpu.VMEM((4, CAP, QW), bf),
            pltpu.VMEM((2, HALF, QW), bf),
            pltpu.VMEM((CAP, TCOL), fl),
            pltpu.VMEM((CAP, TCOL), bf),
            pltpu.VMEM((2, 128, CAP), fl),
            pltpu.VMEM((2, 3, 8, CAP), fl),
            pltpu.SemaphoreType.DMA((SEM_N,)),
            pltpu.SemaphoreType.DMA((SEM_N,)),
            pltpu.SemaphoreType.DMA((5,)),
        ],
        compiler_params=pltpu.CompilerParams(
            collective_id=0, has_side_effects=True, vmem_limit_bytes=60 * 1024 * 1024
        ),
    )(
        tokens,
        w_query,
        w_key,
        w_value,
        w_out.T,
        cos,
        sin,
        first_row[:, None],
        gains,
        out_gain[None, :],
        live_rows,
    )


def solution(mesh):
    in_specs = (
        P("fsdp", "tensor"),
        P("fsdp"),
        P("fsdp"),
        P("fsdp", "tensor"),
        P("fsdp", "tensor"),
        P("fsdp", "tensor"),
        P("tensor", "fsdp"),
        P("tensor"),
        P("tensor"),
        P("tensor"),
    )
    return jax.shard_map(
        body, mesh=mesh, in_specs=in_specs, out_specs=P("fsdp", "tensor"), check_vma=False
    )
```

time: 841 us -> 145 us (0.17)
  waiting for transfers between devices: 667 us -> 0 us
  Pallas kernels: 0 us -> 133 us
  matrix products: 84.7 us -> 0 us
  blocking collectives: 35.3 us -> 0 us
  local copies, waits for them, and re-layouts: 21 us -> 6.42 us
  between operations: 14.4 us -> 0.67 us
  other arithmetic: 16.7 us -> 4.04 us
    all_gather x5 -> x0, waiting for transfers between devices: 573 us -> none  [the longest x1 153 us: layer_rows(): lax.all_gather(w_value, 'fsdp', axis=0, tiled=True)]
    pallas_call x0 -> x1, Pallas kernels: none -> 133 us  [body(): pl.pallas_call(kernel, out_shape=jax.ShapeDtypeStruct((CAP, TCOL), bf), i...]
    reduce_scatter x1 -> x0, waiting for transfers between devices: 91.1 us -> none  [layer_rows(): lax.psum_scatter(partial_value.astype(jnp.bfloat16), 'tensor', scatter_di...]
    dot_general x28 -> x0, matrix products: 84.7 us -> none  [the longest x24 80.8 us: block_step(): jnp.dot(piece, matrix, preferred_element_type=jnp.float32)]
    psum x2 -> x0, blocking collectives: 35.3 us -> none  [the longest x1 28 us: layer_rows(): lax.psum((jnp.sum(query * query, axis=1), jnp.sum(key * key, axis=1)), 't...]
    while x28 -> x0, local copies, waits for them, and re-layouts: 11.7 us -> none  [the longest x4 11.6 us: project(): results = lax.fori_loop(0, counts[pack_index] // BLOCK, block_step, results)]
  transfers between devices with their start and end apart: 6 -> 0, of which waited for: 6 -> 0; matrix products, arithmetic and copies ran while one was open for 9% -> 0% of each run, Pallas kernels for 0% -> 0%
where the time goes in v1:
time: 145 us; the launch traced here: 144 us
  Pallas kernels  133 us (92%)
  local copies, waits for them, and re-layouts  6.42 us (4%)
  other arithmetic  4.04 us (3%)
    pallas_call x1, Pallas kernels, body(): pl.pallas_call(kernel, out_shape=jax.ShapeDtypeStruct((CAP, TCOL), bf), i...  133 us
    unnamed x1, local copies, waits for them, and re-layouts  2.94 us

profile of v1, /device:TPU:1, one launch (start us, length us, event | category | flops | bytes accessed | tf_op | source)
XLA Modules:
  0.0 144.3 jit_solution(7615287908097104922)
XLA Ops:
  0.7 0.7 pad_maximum_fusion.2
  1.4 0.6 broadcast_in_dim.12.gain_ref
  2.0 0.7 subtract_convert_fusion
  2.7 1.3 broadcast_in_dim.13.ogain_ref
  4.0 1.6 %broadcast_in_dim.14.start_ref = s32[768,1]{1,0:T(8,128)} reshape(s32[768]{0:T(1024)} %param.12) | data formatting | bytes 6144 | tf_op jit(solution)/shard_map/broadcast_in_dim | solution.py:477
  5.6 1.4 %fusion = (f32[768,64]{1,0:T(8,128)S(1)}, f32[768,64]{1,0:T(8,128)S(1)}, f32[768,64]{1,0:T(8,128)S(1)}) fusion(f32[64]{0:T(128)S(1)} %negate_power_fusion, f32[768]{0:T(1024)S(1)} %subtract_convert_fusion), kind=kLoop, calls=%fused_computation.4 | loop fusion | flops 98304 | bytes 593152 | tf_op jit(solution)/shard_map/neg | solution.py:437
  7.0 1.2 pad_maximum_fusion
  8.2 133.1 %shard_map.100 = bf16[768,1280]{1,0:T(8,128)(2,1)} custom-call(bf16[768,1280]{1,0:T(8,128)(2,1)} %tok_hbm.1, bf16[160,640]{1,0:T(8,128)(2,1)} %wq_hbm.1, bf16[160,128]{1,0:T(8,128)(2,1)} %wk_hbm.1, bf16[160,128]{1,0:T(8,128)(2,1)} %wv_hbm.1, bf16[160,640]{1,0:T(8,128)(2,1)} %bitcast.1, f32[768,128]{1,0:T(8,128)} %get-tuple-element.8.cos_ref, ...), custom_call_target="tpu_custom_call" | custom-call | tf_op jit(solution)/shard_map/pallas_call | solution.py:443
  141.3 2.9 %copy.14 = bf16[768,1280]{1,0:T(8,128)(2,1)} copy(bf16[768,1280]{1,0:T(8,128)(2,1)} %shard_map.100) | data formatting | bytes 3932160
  (1 shorter events, 0.0 us)

commit v2 on v1

v2 whole, which is shorter than its diff:
```python
import functools
import math

import jax
import jax.numpy as jnp
from jax import lax
from jax.experimental import pallas as pl
from jax.experimental.pallas import tpu as pltpu
from jax.sharding import PartitionSpec as P

D = 5120
HEADS = 20
KV_HEADS = 4
HEAD_DIM = 128
CAP = 768
HALF = 384
EPS = 1e-06
ROPE_BASE = 500000.0
SHARD = 160
QKV = 896
QW = 640
TCOL = 1280
MESH = pl.DeviceIdType.MESH

TOK_CHUNK = 64
TOK_N = CAP // TOK_CHUNK
ATT_CHUNK = 128
ATT_N = CAP // ATT_CHUNK

AG_SEMS = 2 * 24 + 2
SEM_W = 0
SEM_O = SEM_W + AG_SEMS
SEM_T = SEM_O + AG_SEMS
SEM_A = SEM_T + 4 * TOK_N
SEM_S = SEM_A + 4 * ATT_N
SEM_P = SEM_S + 6
SEM_N = SEM_P + 1


def plan(events, rate=45.0, hop=1.8, report=None):
    now, done, arrive, free, order = 0.0, set(), {}, {}, []
    left = list(events)
    while left:
        best = None
        for n, (name, after, waits, sends, cost, late, work) in enumerate(left):
            if any(a not in done for a in after) or any(i not in arrive for i, _ in waits):
                continue
            ready = max([now] + [arrive[i] for i, _ in waits])
            key = (ready, late, n)
            if best is None or key < best[0]:
                best = (key, n)
        (ready, _, _), n = best
        name, after, waits, sends, cost, late, work = left.pop(n)
        now = ready + cost + 0.02
        for idx, link, kb, _ in sends:
            lines = ("y+", "y-") if link == "yp" else (link,)
            begin = max([now] + [free.get(line, 0.0) for line in lines])
            speed = 200.0 if link == "c" else rate
            finish = begin + kb / speed
            for line in lines:
                free[line] = finish if len(lines) == 1 else max(free.get(line, 0.0), finish)
            arrive[idx] = finish + (1.0 if link == "c" else 2 * hop if link == "far" else hop)
        done.add(name)
        order.append(name)
        if report is not None:
            report.append((name, now))
    return order


def kernel(
    tok_hbm,
    wq_hbm,
    wk_hbm,
    wv_hbm,
    wot_hbm,
    cos_ref,
    sin_ref,
    start_ref,
    gain_ref,
    ogain_ref,
    live_ref,
    out_hbm,
    wbuf,
    obuf,
    xall,
    xstage,
    acc,
    rot,
    vbuf,
    att,
    astage,
    oacc,
    res,
    sqt,
    sqr,
    krow,
    qcol,
    send_sem,
    recv_sem,
    local_sem,
):
    f = lax.axis_index("fsdp")
    t = lax.axis_index("tensor")
    x, yl, z = f // 8, (f // 4) % 2, f % 4
    yh, core = t // 2, t % 2
    y = 2 * yh + yl

    def dev(dx=0, dy=0, dz=0, flip=0):
        ny = (y + dy) % 4
        nf = ((x + dx) % 4) * 8 + (ny % 2) * 4 + (z + dz) % 4
        nc = (core + flip) % 2
        return (nf, (ny // 2) * 2 + nc)

    ypair = ((x * 8 + (1 - yl) * 4 + z), t)
    swap_f = t * 8 + yl * 4 + z
    swap = (swap_f, x)
    sends = []

    def send(src, dst, idx, to):
        copy = pltpu.make_async_remote_copy(
            src_ref=src,
            dst_ref=dst,
            send_sem=send_sem.at[idx],
            recv_sem=recv_sem.at[idx],
            device_id=to,
            device_id_type=MESH,
        )
        copy.start()
        sends.append(copy)

    def recv(dst, idx):
        pltpu.make_async_remote_copy(
            src_ref=dst,
            dst_ref=dst,
            send_sem=send_sem.at[idx],
            recv_sem=recv_sem.at[idx],
            device_id=ypair,
            device_id_type=MESH,
        ).wait_recv()

    events = []

    def event(name, after=(), waits=(), sends=(), cost=0.0, late=0, work=None):
        events.append((name, tuple(after), tuple(waits), tuple(sends), cost, late, work))

    def run():
        for name in plan(events):
            _, _, waits, outs, _, _, work = next(e for e in events if e[0] == name)
            for idx, dst in waits:
                recv(dst(), idx)
            if work is not None:
                work()
            for idx, _, _, what in outs:
                what(idx)

    local = [
        pltpu.make_async_copy(wq_hbm, wbuf.at[x, yl, z, :, pl.ds(0, QW)], local_sem.at[0]),
        pltpu.make_async_copy(wk_hbm, wbuf.at[x, yl, z, :, pl.ds(QW, 128)], local_sem.at[1]),
        pltpu.make_async_copy(wv_hbm, wbuf.at[x, yl, z, :, pl.ds(QW + 128, 128)], local_sem.at[2]),
        pltpu.make_async_copy(tok_hbm, xall.at[t], local_sem.at[3]),
    ]
    for copy in local:
        copy.start()

    barrier = pltpu.get_barrier_semaphore()
    partners = [
        dev(dx=1), dev(dx=3), dev(dz=1), dev(dz=3), dev(dy=1), dev(dy=3),
        dev(flip=1), dev(dy=2), dev(dy=2, flip=1),
    ]
    for to in partners:
        pl.semaphore_signal(barrier, inc=1, device_id=to, device_id_type=MESH)

    @pl.when(x != t)
    def _():
        pl.semaphore_signal(barrier, inc=1, device_id=swap, device_id_type=MESH)

    pl.semaphore_wait(barrier, len(partners) + jnp.where(x != t, 1, 0))

    def gather(tag, buf, base, kb, start, start_y):
        order = (0, 3, 1, 2)

        def slot(color, da, yy, db):
            dx, dz = (da, db) if color == 0 else (db, da)
            return buf.at[(x + dx) % 4, yy, (z + dz) % 4, pl.ds(color * 80, 80)]

        def pair(color, da, db):
            dx, dz = (da, db) if color == 0 else (db, da)
            return buf.at[(x + dx) % 4, :, (z + dz) % 4, pl.ds(color * 80, 80)]

        def out(color, stage, sign, k, ref, units=1):
            along_x = (stage == 0) == (color == 0)
            d = sign % 4
            to = dev(dx=d) if along_x else dev(dz=d)
            link = ("x" if along_x else "z") + ("+" if sign > 0 else "-")
            return (base + 24 * color + k, link, units * kb, lambda idx: send(ref(), ref(), idx, to))

        def second(c, k):
            da = order[k]
            return [
                out(c, 1, 1, 6 + 4 * k, lambda: pair(c, da, 0), 2),
                out(c, 1, -1, 7 + 4 * k, lambda: pair(c, da, 0), 2),
            ]

        def half(c, yy):
            return buf.at[x, yy, z, pl.ds(c * 80, 80)]

        for c in range(2):
            event(
                f"{tag}y{c}", start_y,
                sends=[(base + 48 + c, "yp", kb, lambda idx, c=c: send(half(c, yl), half(c, yl), idx, ypair))],
            )
        for stage in range(2):
            for c in range(2):
                k = 0 if stage == 0 else 6
                own = functools.partial(half, c, yl)
                event(
                    f"{tag}0{stage}{c}", start,
                    sends=[out(c, stage, 1, k, own), out(c, stage, -1, k + 1, own)],
                )
        for c in range(2):
            sem = base + 24 * c
            other = functools.partial(half, c, 1 - yl)
            event(
                f"{tag}1{c}", start,
                waits=[(base + 48 + c, other)],
                sends=[
                    out(c, 0, 1, 2, other), out(c, 0, -1, 3, other),
                    out(c, 1, 1, 22, other), out(c, 1, -1, 23, other),
                ],
            )
            event(
                f"{tag}2l{c}",
                waits=[(sem, lambda c=c: slot(c, 3, yl, 0)), (sem + 2, lambda c=c: slot(c, 3, 1 - yl, 0))],
                sends=[out(c, 0, 1, 4, lambda c=c: slot(c, 3, 0, 0))] + second(c, 1),
            )
            event(
                f"{tag}2r{c}",
                waits=[(sem + 1, lambda c=c: slot(c, 1, yl, 0)), (sem + 3, lambda c=c: slot(c, 1, 1 - yl, 0))],
                sends=[out(c, 0, -1, 5, lambda c=c: slot(c, 1, 1, 0))] + second(c, 2),
            )
            event(
                f"{tag}3{c}",
                waits=[(sem + 4, lambda c=c: slot(c, 2, 0, 0)), (sem + 5, lambda c=c: slot(c, 2, 1, 0))],
                sends=second(c, 3),
            )
            for k in range(4):
                da = order[k]
                left = [(sem + 6 + 4 * k, lambda c=c, da=da: pair(c, da, 3))]
                right = [(sem + 7 + 4 * k, lambda c=c, da=da: pair(c, da, 1))]
                if k == 0:
                    left = [
                        (sem + 6, lambda c=c: slot(c, 0, yl, 3)), (sem + 22, lambda c=c: slot(c, 0, 1 - yl, 3)),
                    ]
                    right = [
                        (sem + 7, lambda c=c: slot(c, 0, yl, 1)), (sem + 23, lambda c=c: slot(c, 0, 1 - yl, 1)),
                    ]
                event(
                    f"{tag}4l{c}{k}", waits=left,
                    sends=[out(c, 1, 1, 8 + 4 * k, lambda c=c, da=da: slot(c, da, 0, 3))],
                )
                event(
                    f"{tag}4r{c}{k}", waits=right,
                    sends=[out(c, 1, -1, 9 + 4 * k, lambda c=c, da=da: slot(c, da, 1, 1))],
                )
                event(
                    f"{tag}5{c}{k}",
                    waits=[
                        (sem + 8 + 4 * k, lambda c=c, da=da: slot(c, da, 0, 2)),
                        (sem + 9 + 4 * k, lambda c=c, da=da: slot(c, da, 1, 2)),
                    ],
                )

    def plane(tag, dx):
        k = (0, 3, 1, 2).index(dx)
        need = [f"{tag}4l0{k}", f"{tag}4r0{k}", f"{tag}50{k}", f"{tag}2l0", f"{tag}2r0", f"{tag}30"]
        if dx == 0:
            need += [f"{tag}11", f"{tag}2l1", f"{tag}2r1", f"{tag}31"]
        else:
            need += [f"{tag}" + {3: "4l1", 1: "4r1", 2: "51"}[dx] + f"{n}" for n in range(4)]
        return need + [f"{tag}10", f"{tag}11"]

    def spread(tag, buf, stage, base, chunk, i, kb, after, src=None):
        rows = pl.ds(i * chunk, chunk)
        held = stage.at[i % 2, pl.ds((i // 2) * chunk, chunk)]
        own = buf.at[t, rows] if src is None else src.at[rows]
        d, back, link = (1, 3, "y+") if i % 2 == 0 else (3, 1, "y-")
        came = (((y + back) % 4) // 2) * 2 + core
        far = (t + 2) % 4
        sib = (core + 1) % 2
        base = base + 4 * i
        event(
            f"{tag}o{i}", after,
            sends=[
                (base, link, kb, lambda idx: send(own, held, idx, dev(dy=d))),
                (base + 1, "c", kb, lambda idx: send(own, buf.at[t, rows], idx, dev(flip=1))),
            ],
        )
        event(
            f"{tag}r{i}", waits=[(base, lambda: held)],
            sends=[(base + 2, link, kb, lambda idx: send(held, buf.at[came, rows], idx, dev(dy=d)))],
        )
        event(
            f"{tag}i{i}", waits=[(base + 2, lambda: buf.at[far, rows])],
            sends=[(base + 3, "c", kb, lambda idx: send(buf.at[far, rows], buf.at[far, rows], idx, dev(flip=1)))],
        )
        event(
            f"{tag}d{i}",
            waits=[
                (base + 1, lambda: buf.at[yh * 2 + sib, rows]),
                (base + 3, lambda: buf.at[(1 - yh) * 2 + sib, rows]),
            ],
        )

    def exchange(k, after):
        outs = []
        for n, to in enumerate((dev(flip=1), dev(dy=2), dev(dy=2, flip=1))):
            outs.append((
                SEM_S + 3 * k + n, "c" if n == 0 else "far", 12,
                lambda idx, n=n, to=to: send(sqt.at[k, pl.ds(0, 8)], sqr.at[k, n], idx, to),
            ))
        event(f"x{k}", after, sends=outs)

    def exchanged(k):
        return [(SEM_S + 3 * k + n, lambda n=n: sqr.at[k, n]) for n in range(3)]

    def total(k):
        return sqt[k, pl.ds(0, 8)] + sqr[k, 0] + sqr[k, 1] + sqr[k, 2]

    def qkv(p, dx, first):
        j = (x + dx) % 4
        rows = pl.ds(p * HALF, HALF)
        part = jnp.dot(
            xall[j, rows], wbuf[j].reshape(TCOL, QKV), preferred_element_type=jnp.float32
        )
        if first:
            acc[rows] = part
        else:
            acc[rows] += part

    lane = lax.broadcasted_iota(jnp.int32, (HALF, 128), 1)

    def sums(p):
        rows = pl.ds(p * HALF, HALF)
        q = acc[rows, pl.ds(0, QW)]
        k = acc[rows, pl.ds(QW, 128)]
        qs = jnp.sum(q * q, axis=1, keepdims=True)
        ks = jnp.sum(k * k, axis=1, keepdims=True)
        both = jnp.where(lane < 4, qs, ks)
        sqt[0, :, rows] = both.T

    def rotate(p):
        rows = pl.ds(p * HALF, HALF)
        for h in range(6):
            cols = pl.ds(h * 128, 128)
            u = acc[rows, cols] * gain_ref[:, cols]
            r = u * cos_ref[rows] + pltpu.roll(u, 64, 1) * sin_ref[rows]
            rot[rows, cols] = r.astype(jnp.bfloat16)
        vbuf[rows] = acc[rows, pl.ds(QW + 128, 128)].astype(jnp.bfloat16)

    def scales():
        sq = total(0)
        res_q = lax.rsqrt(sq[0:4] / (HEADS * HEAD_DIM) + EPS) * (1.0 / math.sqrt(HEAD_DIM))
        res_k = lax.rsqrt(sq[4:8] / (KV_HEADS * HEAD_DIM) + EPS)
        both = jnp.concatenate([res_q, res_k], axis=0)
        krow[...] = both
        qcol[...] = jnp.concatenate([both] * 16, axis=0).T

    def attend(p, b):
        rows = pl.ds(p * HALF + b * 128, 128)
        width = (b + 1) * 128
        seen = pl.ds(p * HALF, width)
        kk = rot[seen, pl.ds(QW, 128)]
        vv = vbuf[seen]
        first = start_ref[rows] - p * HALF
        col = lax.broadcasted_iota(jnp.int32, (128, width), 1)
        row = lax.broadcasted_iota(jnp.int32, (128, width), 0) + b * 128
        allowed = (col >= first) & (col <= row)
        scale = qcol[rows, 0:1] * krow[4:5, p * HALF : p * HALF + width]
        for h in range(5):
            cols = pl.ds(h * 128, 128)
            s = lax.dot_general(
                rot[rows, cols], kk, (((1,), (1,)), ((), ())), preferred_element_type=jnp.float32
            )
            s = jnp.where(allowed, s * scale, jnp.float32(-1e30))
            e = jnp.exp(s - jnp.max(s, axis=1, keepdims=True))
            probs = (e * (1.0 / jnp.sum(e, axis=1, keepdims=True))).astype(jnp.bfloat16)
            o = jnp.dot(probs, vv, preferred_element_type=jnp.float32)
            att[t, rows, cols] = o.astype(jnp.bfloat16)

    def project(p, dx, first):
        j = (x + dx) % 4
        rows = pl.ds(p * HALF, HALF)
        part = lax.dot_general(
            att[j, rows],
            obuf[j].reshape(TCOL, QW),
            (((1,), (1,)), ((), ())),
            preferred_element_type=jnp.float32,
        )
        if first:
            oacc[rows] = part
        else:
            oacc[rows] += part

    def out_sums(p):
        rows = pl.ds(p * HALF, HALF)
        o = oacc[rows]
        sqt[1, :, rows] = jnp.broadcast_to(jnp.sum(o * o, axis=1, keepdims=True), (HALF, 128)).T

    def finish():
        sums_out = jnp.concatenate([total(1)] * 16, axis=0).T
        live = live_ref[0]
        for p in range(2):
            rows = pl.ds(p * HALF, HALF)
            scale = lax.rsqrt(sums_out[p * HALF : (p + 1) * HALF, 0:1] / D + EPS)
            r = xall[t, rows].astype(jnp.float32) + oacc[rows] * scale * ogain_ref[...]
            row = lax.broadcasted_iota(jnp.int32, (HALF, TCOL), 0) + p * HALF
            res[rows] = jnp.where(row < live, r, 0.0).astype(jnp.bfloat16)
        done = pltpu.make_async_copy(res, out_hbm, local_sem.at[0])
        done.start()
        done.wait()

    for copy in local[:3]:
        copy.wait()

    own_o = obuf.at[x, yl, z]

    def swap_out():
        @pl.when(x != t)
        def _():
            copy = pltpu.make_async_remote_copy(
                src_ref=wot_hbm, dst_ref=obuf.at[t, yl, z], send_sem=send_sem.at[SEM_P],
                recv_sem=recv_sem.at[SEM_P], device_id=swap, device_id_type=MESH,
            )
            copy.start()

        @pl.when(x == t)
        def _():
            copy = pltpu.make_async_copy(wot_hbm, own_o, local_sem.at[4])
            copy.start()

    def swap_in():
        @pl.when(x != t)
        def _():
            copy = pltpu.make_async_remote_copy(
                src_ref=wot_hbm, dst_ref=own_o, send_sem=send_sem.at[SEM_P],
                recv_sem=recv_sem.at[SEM_P], device_id=swap, device_id_type=MESH,
            )
            copy.wait()

        @pl.when(x == t)
        def _():
            copy = pltpu.make_async_copy(wot_hbm, own_o, local_sem.at[4])
            copy.wait()

    w_sends = [f"w4{s}{c}{k}" for s in "lr" for c in range(2) for k in range(4)]
    gather("w", wbuf, SEM_W, 143.4, (), ())
    event("swap", ("w010", "w011"), sends=[(SEM_P, "far", 205, lambda idx: swap_out())])
    for i in range(TOK_N):
        spread("t", xall, xstage, SEM_T, TOK_CHUNK, i, 163.8, ("wy0", "wy1", "w010", "w011"), tok_hbm)
    event("swapped", ("swap", "tr5"), cost=0.1, work=swap_in)
    gather("o", obuf, SEM_O, 102.4, ["swapped"] + w_sends, ["swapped"])
    event("own", work=local[3].wait)

    half_t = TOK_N // 2
    last = {}
    for p in range(2):
        rows_in = ["own"] + [f"t{s}{p * half_t + i}" for s in "rid" for i in range(half_t)]
        for n, dx in enumerate((0, 3, 1, 2)):
            event(
                f"q{p}{n}", rows_in + plane("w", dx) + ([f"q{p}{n - 1}"] if n else []),
                cost=1.2, late=1, work=functools.partial(qkv, p, dx, n == 0),
            )
        event(f"sum{p}", [f"q{p}3"], cost=0.4, late=1, work=functools.partial(sums, p))
    exchange(0, ("sum0", "sum1"))
    for p in range(2):
        event(f"rot{p}", ("x0",), cost=1.0, late=1, work=functools.partial(rotate, p))
    event("scale", ("rot0", "rot1"), waits=exchanged(0), cost=0.4, late=1, work=scales)
    prev = "scale"
    half_a = ATT_N // 2
    for i in range(ATT_N):
        event(f"att{i}", (prev,), cost=0.8, late=1, work=functools.partial(attend, i // 3, i % 3))
        spread("a", att, astage, SEM_A, ATT_CHUNK, i, 163.8, (f"att{i}",))
        prev = f"att{i}"
    for p in range(2):
        rows_in = [f"a{s}{p * half_a + i}" for s in "orid" for i in range(half_a)]
        for n, dx in enumerate((0, 3, 1, 2)):
            event(
                f"p{p}{n}", rows_in + plane("o", dx) + ([f"p{p}{n - 1}"] if n else []),
                cost=0.9, late=1, work=functools.partial(project, p, dx, n == 0),
            )
        event(f"osum{p}", [f"p{p}3"], cost=0.3, late=1, work=functools.partial(out_sums, p))
    exchange(1, ("osum0", "osum1"))
    event("end", ("x1",), waits=exchanged(1), cost=3.0, late=1, work=finish)
    run()
    for copy in sends:
        copy.wait_send()


def body(
    tokens, live_rows, first_row, w_query, w_key, w_value, w_out, query_gain, key_gain, out_gain
):
    half = HEAD_DIM // 2
    freqs = jnp.power(ROPE_BASE, -(jnp.arange(half, dtype=jnp.float32) * 2.0 / HEAD_DIM))
    positions = (jnp.arange(CAP, dtype=jnp.int32) - first_row).astype(jnp.float32)
    angle = positions[:, None] * freqs[None, :]
    cosine, sine = jnp.cos(angle), jnp.sin(angle)
    cos = jnp.concatenate([cosine, cosine], axis=1)
    sin = jnp.concatenate([-sine, sine], axis=1)
    gains = jnp.concatenate([query_gain, key_gain])[None, :]
    hbm = pl.BlockSpec(memory_space=pl.ANY)
    vmem = pl.BlockSpec(memory_space=pltpu.VMEM)
    smem = pl.BlockSpec(memory_space=pltpu.SMEM)
    bf, fl = jnp.bfloat16, jnp.float32
    return pl.pallas_call(
        kernel,
        out_shape=jax.ShapeDtypeStruct((CAP, TCOL), bf),
        in_specs=[hbm] * 5 + [vmem] * 5 + [smem],
        out_specs=hbm,
        scratch_shapes=[
            pltpu.VMEM((4, 2, 4, SHARD, QKV), bf),
            pltpu.VMEM((4, 2, 4, SHARD, QW), bf),
            pltpu.VMEM((4, CAP, TCOL), bf),
            pltpu.VMEM((2, HALF, TCOL), bf),
            pltpu.VMEM((CAP, QKV), fl),
            pltpu.VMEM((CAP, QW + 128), bf),
            pltpu.VMEM((CAP, 128), bf),
            pltpu.VMEM((4, CAP, QW), bf),
            pltpu.VMEM((2, HALF, QW), bf),
            pltpu.VMEM((CAP, TCOL), fl),
            pltpu.VMEM((CAP, TCOL), bf),
            pltpu.VMEM((2, 128, CAP), fl),
            pltpu.VMEM((2, 3, 8, CAP), fl),
            pltpu.VMEM((8, CAP), fl),
            pltpu.VMEM((CAP, 128), fl),
            pltpu.SemaphoreType.DMA((SEM_N,)),
            pltpu.SemaphoreType.DMA((SEM_N,)),
            pltpu.SemaphoreType.DMA((5,)),
        ],
        compiler_params=pltpu.CompilerParams(
            collective_id=0, has_side_effects=True, vmem_limit_bytes=60 * 1024 * 1024
        ),
    )(
        tokens,
        w_query,
        w_key,
        w_value,
        w_out.T,
        cos,
        sin,
        first_row[:, None],
        gains,
        out_gain[None, :],
        live_rows,
    )


def solution(mesh):
    in_specs = (
        P("fsdp", "tensor"),
        P("fsdp"),
        P("fsdp"),
        P("fsdp", "tensor"),
        P("fsdp", "tensor"),
        P("fsdp", "tensor"),
        P("tensor", "fsdp"),
        P("tensor"),
        P("tensor"),
        P("tensor"),
    )
    return jax.shard_map(
        body, mesh=mesh, in_specs=in_specs, out_specs=P("fsdp", "tensor"), check_vma=False
    )
```

time: 145 us -> 135 us (0.931)
  Pallas kernels: 133 us -> 124 us
    pallas_call x1, Pallas kernels: 133 us -> 124 us  [body(): pl.pallas_call(kernel, out_shape=jax.ShapeDtypeStruct((CAP, TCOL), bf), i...]
where the time goes in v2:
time: 135 us
  Pallas kernels  124 us (92%)
  local copies, waits for them, and re-layouts  6.42 us (5%)
  other arithmetic  4.04 us (3%)
    pallas_call x1, Pallas kernels, body(): pl.pallas_call(kernel, out_shape=jax.ShapeDtypeStruct((CAP, TCOL), bf), i...  124 us
    unnamed x1, local copies, waits for them, and re-layouts  2.94 us

profile of v2, /device:TPU:1, one launch (start us, length us, event | category | flops | bytes accessed | tf_op | source)
XLA Modules:
  0.0 135.0 jit_solution(205423962469679636)
XLA Ops:
  0.7 0.7 pad_maximum_fusion.2
  1.4 0.6 broadcast_in_dim.12.gain_ref
  2.0 0.7 subtract_convert_fusion
  2.7 1.3 broadcast_in_dim.13.ogain_ref
  4.0 1.6 %broadcast_in_dim.14.start_ref = s32[768,1]{1,0:T(8,128)} reshape(s32[768]{0:T(1024)} %param.12) | data formatting | bytes 6144 | tf_op jit(solution)/shard_map/broadcast_in_dim | solution.py:550
  5.6 1.4 %fusion = (f32[768,64]{1,0:T(8,128)S(1)}, f32[768,64]{1,0:T(8,128)S(1)}, f32[768,64]{1,0:T(8,128)S(1)}) fusion(f32[64]{0:T(128)S(1)} %negate_power_fusion, f32[768]{0:T(1024)S(1)} %subtract_convert_fusion), kind=kLoop, calls=%fused_computation.4 | loop fusion | flops 98304 | bytes 593152 | tf_op jit(solution)/shard_map/neg | solution.py:508
  7.0 1.2 pad_maximum_fusion
  8.2 123.9 %shard_map.100 = bf16[768,1280]{1,0:T(8,128)(2,1)} custom-call(bf16[768,1280]{1,0:T(8,128)(2,1)} %tok_hbm.1, bf16[160,640]{1,0:T(8,128)(2,1)} %wq_hbm.1, bf16[160,128]{1,0:T(8,128)(2,1)} %wk_hbm.1, bf16[160,128]{1,0:T(8,128)(2,1)} %wv_hbm.1, bf16[160,640]{1,0:T(8,128)(2,1)} %bitcast.1, f32[768,128]{1,0:T(8,128)} %get-tuple-element.8.cos_ref, ...), custom_call_target="tpu_custom_call" | custom-call | tf_op jit(solution)/shard_map/pallas_call | solution.py:514
  132.1 2.9 %copy.14 = bf16[768,1280]{1,0:T(8,128)(2,1)} copy(bf16[768,1280]{1,0:T(8,128)(2,1)} %shard_map.100) | data formatting | bytes 3932160
  (1 shorter events, 0.0 us)

commit v3 on v2

--- a/solution.py
+++ b/solution.py
@@ -33,7 +33,7 @@
 SEM_T = SEM_O + AG_SEMS
 SEM_A = SEM_T + 4 * TOK_N
 SEM_S = SEM_A + 4 * ATT_N
-SEM_P = SEM_S + 6
+SEM_P = SEM_S + 12
 SEM_N = SEM_P + 1
 
 
@@ -53,12 +53,17 @@
         name, after, waits, sends, cost, late, work = left.pop(n)
         now = ready + cost + 0.02
         for idx, link, kb, _ in sends:
-            lines = ("y+", "y-") if link == "yp" else (link,)
+            lines = {"yp": ("y+", "y-"), "far": ()}.get(link, (link,))
             begin = max([now] + [free.get(line, 0.0) for line in lines])
-            speed = 200.0 if link == "c" else rate
-            finish = begin + kb / speed
+            if link == "far" and kb < 100:
+                begin = max(now, min(free.get("y+", 0.0), free.get("y-", 0.0)))
+            if link == "c":
+                busy = finish = begin + kb / 200.0
+            else:
+                finish = begin + kb / rate
+                busy = max(finish, begin + kb / (2 * rate) + hop)
             for line in lines:
-                free[line] = finish if len(lines) == 1 else max(free.get(line, 0.0), finish)
+                free[line] = busy
             arrive[idx] = finish + (1.0 if link == "c" else 2 * hop if link == "far" else hop)
         done.add(name)
         order.append(name)
@@ -153,6 +158,13 @@
             for idx, _, _, what in outs:
                 what(idx)
 
+    written = [
+        pltpu.make_async_copy(
+            res.at[pl.ds(p * HALF, HALF)], out_hbm.at[pl.ds(p * HALF, HALF)], local_sem.at[p]
+        )
+        for p in range(2)
+    ]
+
     local = [
         pltpu.make_async_copy(wq_hbm, wbuf.at[x, yl, z, :, pl.ds(0, QW)], local_sem.at[0]),
         pltpu.make_async_copy(wk_hbm, wbuf.at[x, yl, z, :, pl.ds(QW, 128)], local_sem.at[1]),
@@ -176,7 +188,7 @@
 
     pl.semaphore_wait(barrier, len(partners) + jnp.where(x != t, 1, 0))
 
-    def gather(tag, buf, base, kb, start, start_y):
+    def gather(tag, buf, base, kb, start, start_y, paired):
         order = (0, 3, 1, 2)
 
         def slot(color, da, yy, db):
@@ -213,29 +225,33 @@
             for c in range(2):
                 k = 0 if stage == 0 else 6
                 own = functools.partial(half, c, yl)
-                event(
-                    f"{tag}0{stage}{c}", start,
-                    sends=[out(c, stage, 1, k, own), out(c, stage, -1, k + 1, own)],
-                )
+                if not paired:
+                    event(
+                        f"{tag}0{stage}{c}", start,
+                        sends=[out(c, stage, 1, k, own), out(c, stage, -1, k + 1, own)],
+                    )
         for c in range(2):
             sem = base + 24 * c
             other = functools.partial(half, c, 1 - yl)
-            event(
-                f"{tag}1{c}", start,
-                waits=[(base + 48 + c, other)],
-                sends=[
+            both = functools.partial(pair, c, 0, 0)
+            if paired:
+                first = [out(c, 0, 1, 0, both, 2), out(c, 0, -1, 1, both, 2)] + second(c, 0)
+                left0 = [(sem, lambda c=c: pair(c, 3, 0))]
+                right0 = [(sem + 1, lambda c=c: pair(c, 1, 0))]
+            else:
+                first = [
                     out(c, 0, 1, 2, other), out(c, 0, -1, 3, other),
                     out(c, 1, 1, 22, other), out(c, 1, -1, 23, other),
-                ],
-            )
+                ]
+                left0 = [(sem, lambda c=c: slot(c, 3, yl, 0)), (sem + 2, lambda c=c: slot(c, 3, 1 - yl, 0))]
+                right0 = [(sem + 1, lambda c=c: slot(c, 1, yl, 0)), (sem + 3, lambda c=c: slot(c, 1, 1 - yl, 0))]
+            event(f"{tag}1{c}", start, waits=[(base + 48 + c, other)], sends=first)
             event(
-                f"{tag}2l{c}",
-                waits=[(sem, lambda c=c: slot(c, 3, yl, 0)), (sem + 2, lambda c=c: slot(c, 3, 1 - yl, 0))],
+                f"{tag}2l{c}", waits=left0,
                 sends=[out(c, 0, 1, 4, lambda c=c: slot(c, 3, 0, 0))] + second(c, 1),
             )
             event(
-                f"{tag}2r{c}",
-                waits=[(sem + 1, lambda c=c: slot(c, 1, yl, 0)), (sem + 3, lambda c=c: slot(c, 1, 1 - yl, 0))],
+                f"{tag}2r{c}", waits=right0,
                 sends=[out(c, 0, -1, 5, lambda c=c: slot(c, 1, 1, 0))] + second(c, 2),
             )
             event(
@@ -245,30 +261,31 @@
             )
             for k in range(4):
                 da = order[k]
-                left = [(sem + 6 + 4 * k, lambda c=c, da=da: pair(c, da, 3))]
-                right = [(sem + 7 + 4 * k, lambda c=c, da=da: pair(c, da, 1))]
-                if k == 0:
+                near_l = functools.partial(pair, c, da, 3)
+                near_r = functools.partial(pair, c, da, 1)
+                far = functools.partial(pair, c, da, 2)
+                left = [(sem + 6 + 4 * k, near_l)]
+                right = [(sem + 7 + 4 * k, near_r)]
+                if k == 0 and not paired:
                     left = [
                         (sem + 6, lambda c=c: slot(c, 0, yl, 3)), (sem + 22, lambda c=c: slot(c, 0, 1 - yl, 3)),
                     ]
                     right = [
                         (sem + 7, lambda c=c: slot(c, 0, yl, 1)), (sem + 23, lambda c=c: slot(c, 0, 1 - yl, 1)),
                     ]
-                event(
-                    f"{tag}4l{c}{k}", waits=left,
-                    sends=[out(c, 1, 1, 8 + 4 * k, lambda c=c, da=da: slot(c, da, 0, 3))],
-                )
-                event(
-                    f"{tag}4r{c}{k}", waits=right,
-                    sends=[out(c, 1, -1, 9 + 4 * k, lambda c=c, da=da: slot(c, da, 1, 1))],
-                )
-                event(
-                    f"{tag}5{c}{k}",
-                    waits=[
-                        (sem + 8 + 4 * k, lambda c=c, da=da: slot(c, da, 0, 2)),
-                        (sem + 9 + 4 * k, lambda c=c, da=da: slot(c, da, 1, 2)),
-                    ],
-                )
+                on_l = [out(c, 1, 1, 8 + 4 * k, lambda c=c, da=da: slot(c, da, 0, 3))]
+                on_r = [out(c, 1, -1, 9 + 4 * k, lambda c=c, da=da: slot(c, da, 1, 1))]
+                end = [
+                    (sem + 8 + 4 * k, lambda c=c, da=da: slot(c, da, 0, 2)),
+                    (sem + 9 + 4 * k, lambda c=c, da=da: slot(c, da, 1, 2)),
+                ]
+                if k == 0:
+                    on_l, on_r, end = [out(c, 1, 1, 8, near_l, 2)], [], [(sem + 8, far)]
+                if k == 1:
+                    on_l, on_r, end = [], [out(c, 1, -1, 13, near_r, 2)], [(sem + 13, far)]
+                event(f"{tag}4l{c}{k}", waits=left, sends=on_l)
+                event(f"{tag}4r{c}{k}", waits=right, sends=on_r)
+                event(f"{tag}5{c}{k}", waits=end)
 
     def plane(tag, dx):
         k = (0, 3, 1, 2).index(dx)
@@ -311,24 +328,25 @@
             ],
         )
 
-    def exchange(k, after):
+    def exchange(k, p, after):
+        cols = pl.ds(p * HALF, HALF)
         outs = []
         for n, to in enumerate((dev(flip=1), dev(dy=2), dev(dy=2, flip=1))):
             outs.append((
-                SEM_S + 3 * k + n, "c" if n == 0 else "far", 12,
-                lambda idx, n=n, to=to: send(sqt.at[k, pl.ds(0, 8)], sqr.at[k, n], idx, to),
+                SEM_S + 6 * k + 3 * p + n, "c" if n == 0 else "far", 12,
+                lambda idx, n=n, to=to: send(sqt.at[k, p, pl.ds(0, 8)], sqr.at[k, p, n], idx, to),
             ))
-        event(f"x{k}", after, sends=outs)
-
-    def exchanged(k):
-        return [(SEM_S + 3 * k + n, lambda n=n: sqr.at[k, n]) for n in range(3)]
-
-    def total(k):
-        return sqt[k, pl.ds(0, 8)] + sqr[k, 0] + sqr[k, 1] + sqr[k, 2]
-
-    def qkv(p, dx, first):
+        event(f"x{k}{p}", after, sends=outs)
+
+    def exchanged(k, p):
+        return [(SEM_S + 6 * k + 3 * p + n, lambda n=n: sqr.at[k, p, n]) for n in range(3)]
+
+    def total(k, p):
+        return sqt[k, p, pl.ds(0, 8)] + sqr[k, p, 0] + sqr[k, p, 1] + sqr[k, p, 2]
+
+    def qkv(row, size, dx, first):
         j = (x + dx) % 4
-        rows = pl.ds(p * HALF, HALF)
+        rows = pl.ds(row, size)
         part = jnp.dot(
             xall[j, rows], wbuf[j].reshape(TCOL, QKV), preferred_element_type=jnp.float32
         )
@@ -346,7 +364,7 @@
         qs = jnp.sum(q * q, axis=1, keepdims=True)
         ks = jnp.sum(k * k, axis=1, keepdims=True)
         both = jnp.where(lane < 4, qs, ks)
-        sqt[0, :, rows] = both.T
+        sqt[0, p] = both.T
 
     def rotate(p):
         rows = pl.ds(p * HALF, HALF)
@@ -354,38 +372,39 @@
             cols = pl.ds(h * 128, 128)
             u = acc[rows, cols] * gain_ref[:, cols]
             r = u * cos_ref[rows] + pltpu.roll(u, 64, 1) * sin_ref[rows]
-            rot[rows, cols] = r.astype(jnp.bfloat16)
+            rot[h, rows] = r.astype(jnp.bfloat16)
         vbuf[rows] = acc[rows, pl.ds(QW + 128, 128)].astype(jnp.bfloat16)
 
-    def scales():
-        sq = total(0)
+    def scales(p):
+        sq = total(0, p)
         res_q = lax.rsqrt(sq[0:4] / (HEADS * HEAD_DIM) + EPS) * (1.0 / math.sqrt(HEAD_DIM))
         res_k = lax.rsqrt(sq[4:8] / (KV_HEADS * HEAD_DIM) + EPS)
         both = jnp.concatenate([res_q, res_k], axis=0)
-        krow[...] = both
-        qcol[...] = jnp.concatenate([both] * 16, axis=0).T
+        krow[p] = both
+        qcol[p] = jnp.concatenate([both] * 16, axis=0).T
 
     def attend(p, b):
         rows = pl.ds(p * HALF + b * 128, 128)
         width = (b + 1) * 128
         seen = pl.ds(p * HALF, width)
-        kk = rot[seen, pl.ds(QW, 128)]
-        vv = vbuf[seen]
         first = start_ref[rows] - p * HALF
         col = lax.broadcasted_iota(jnp.int32, (128, width), 1)
         row = lax.broadcasted_iota(jnp.int32, (128, width), 0) + b * 128
-        allowed = (col >= first) & (col <= row)
-        scale = qcol[rows, 0:1] * krow[4:5, p * HALF : p * HALF + width]
+        bias = jnp.where((col >= first) & (col <= row), 0.0, -1e30).astype(jnp.float32)
+        scale = qcol[p, pl.ds(b * 128, 128), 0:1] * krow[p, 4:5, 0:width]
+        s = lax.dot_general(
+            rot[0:5, rows].reshape(QW, 128), rot[5, seen], (((1,), (1,)), ((), ())),
+            preferred_element_type=jnp.float32,
+        ).reshape(5, 128, width)
+        s = s * scale[None] + bias[None]
+        e = jnp.exp(s - jnp.max(s, axis=2, keepdims=True))
+        inv = 1.0 / jnp.sum(e, axis=2, keepdims=True)
+        o = jnp.dot(
+            e.astype(jnp.bfloat16).reshape(QW, width), vbuf[seen], preferred_element_type=jnp.float32
+        ).reshape(5, 128, 128)
+        o = (o * inv).astype(jnp.bfloat16)
         for h in range(5):
-            cols = pl.ds(h * 128, 128)
-            s = lax.dot_general(
-                rot[rows, cols], kk, (((1,), (1,)), ((), ())), preferred_element_type=jnp.float32
-            )
-            s = jnp.where(allowed, s * scale, jnp.float32(-1e30))
-            e = jnp.exp(s - jnp.max(s, axis=1, keepdims=True))
-            probs = (e * (1.0 / jnp.sum(e, axis=1, keepdims=True))).astype(jnp.bfloat16)
-            o = jnp.dot(probs, vv, preferred_element_type=jnp.float32)
-            att[t, rows, cols] = o.astype(jnp.bfloat16)
+            att[t, rows, pl.ds(h * 128, 128)] = o[h]
 
     def project(p, dx, first):
         j = (x + dx) % 4
@@ -404,20 +423,16 @@
     def out_sums(p):
         rows = pl.ds(p * HALF, HALF)
         o = oacc[rows]
-        sqt[1, :, rows] = jnp.broadcast_to(jnp.sum(o * o, axis=1, keepdims=True), (HALF, 128)).T
-
-    def finish():
-        sums_out = jnp.concatenate([total(1)] * 16, axis=0).T
-        live = live_ref[0]
-        for p in range(2):
-            rows = pl.ds(p * HALF, HALF)
-            scale = lax.rsqrt(sums_out[p * HALF : (p + 1) * HALF, 0:1] / D + EPS)
-            r = xall[t, rows].astype(jnp.float32) + oacc[rows] * scale * ogain_ref[...]
-            row = lax.broadcasted_iota(jnp.int32, (HALF, TCOL), 0) + p * HALF
-            res[rows] = jnp.where(row < live, r, 0.0).astype(jnp.bfloat16)
-        done = pltpu.make_async_copy(res, out_hbm, local_sem.at[0])
-        done.start()
-        done.wait()
+        sqt[1, p] = jnp.broadcast_to(jnp.sum(o * o, axis=1, keepdims=True), (HALF, 128)).T
+
+    def finish(p):
+        sums_out = jnp.concatenate([total(1, p)] * 16, axis=0).T
+        rows = pl.ds(p * HALF, HALF)
+        scale = lax.rsqrt(sums_out[:, 0:1] / D + EPS)
+        r = xall[t, rows].astype(jnp.float32) + oacc[rows] * scale * ogain_ref[...]
+        row = lax.broadcasted_iota(jnp.int32, (HALF, TCOL), 0) + p * HALF
+        res[rows] = jnp.where(row < live_ref[0], r, 0.0).astype(jnp.bfloat16)
+        written[p].start()
 
     for copy in local[:3]:
         copy.wait()
@@ -453,45 +468,47 @@
             copy.wait()
 
     w_sends = [f"w4{s}{c}{k}" for s in "lr" for c in range(2) for k in range(4)]
-    gather("w", wbuf, SEM_W, 143.4, (), ())
+    gather("w", wbuf, SEM_W, 143.4, (), (), False)
     event("swap", ("w010", "w011"), sends=[(SEM_P, "far", 205, lambda idx: swap_out())])
     for i in range(TOK_N):
         spread("t", xall, xstage, SEM_T, TOK_CHUNK, i, 163.8, ("wy0", "wy1", "w010", "w011"), tok_hbm)
     event("swapped", ("swap", "tr5"), cost=0.1, work=swap_in)
-    gather("o", obuf, SEM_O, 102.4, ["swapped"] + w_sends, ["swapped"])
+    gather("o", obuf, SEM_O, 102.4, ["swapped"] + w_sends, ["swapped"], True)
     event("own", work=local[3].wait)
 
-    half_t = TOK_N // 2
-    last = {}
     for p in range(2):
-        rows_in = ["own"] + [f"t{s}{p * half_t + i}" for s in "rid" for i in range(half_t)]
-        for n, dx in enumerate((0, 3, 1, 2)):
-            event(
-                f"q{p}{n}", rows_in + plane("w", dx) + ([f"q{p}{n - 1}"] if n else []),
-                cost=1.2, late=1, work=functools.partial(qkv, p, dx, n == 0),
-            )
-        event(f"sum{p}", [f"q{p}3"], cost=0.4, late=1, work=functools.partial(sums, p))
-    exchange(0, ("sum0", "sum1"))
-    for p in range(2):
-        event(f"rot{p}", ("x0",), cost=1.0, late=1, work=functools.partial(rotate, p))
-    event("scale", ("rot0", "rot1"), waits=exchanged(0), cost=0.4, late=1, work=scales)
-    prev = "scale"
+        blocks = [(0, HALF)] if p == 0 else [(HALF, HALF // 2), (HALF + HALF // 2, HALF // 2)]
+        for m, (row, size) in enumerate(blocks):
+            chunks = range(row // TOK_CHUNK, (row + size) // TOK_CHUNK)
+            rows_in = ["own"] + [f"t{s}{i}" for s in "rid" for i in chunks]
+            for n, dx in enumerate((0, 3, 1, 2)):
+                event(
+                    f"q{p}{m}{n}", rows_in + plane("w", dx) + ([f"q{p}{m}{n - 1}"] if n else []),
+                    cost=1.25 * size / HALF, late=1, work=functools.partial(qkv, row, size, dx, n == 0),
+                )
+        event(f"sum{p}", [f"q{p}{m}3" for m in range(len(blocks))], cost=0.2, late=1, work=functools.partial(sums, p))
+        exchange(0, p, [f"sum{p}"])
+        event(f"rot{p}", [f"x0{p}"], cost=0.4, late=1, work=functools.partial(rotate, p))
+        event(f"scale{p}", [f"rot{p}"], waits=exchanged(0, p), cost=0.2, late=1, work=functools.partial(scales, p))
     half_a = ATT_N // 2
     for i in range(ATT_N):
-        event(f"att{i}", (prev,), cost=0.8, late=1, work=functools.partial(attend, i // 3, i % 3))
+        p, b = i // 3, i % 3
+        prev = f"att{i - 1}" if b else f"scale{p}"
+        event(f"att{i}", (prev,), cost=0.6 + 0.4 * b, late=0.5 + p, work=functools.partial(attend, p, b))
         spread("a", att, astage, SEM_A, ATT_CHUNK, i, 163.8, (f"att{i}",))
-        prev = f"att{i}"
     for p in range(2):
         rows_in = [f"a{s}{p * half_a + i}" for s in "orid" for i in range(half_a)]
         for n, dx in enumerate((0, 3, 1, 2)):
             event(
                 f"p{p}{n}", rows_in + plane("o", dx) + ([f"p{p}{n - 1}"] if n else []),
-                cost=0.9, late=1, work=functools.partial(project, p, dx, n == 0),
-            )
-        event(f"osum{p}", [f"p{p}3"], cost=0.3, late=1, work=functools.partial(out_sums, p))
-    exchange(1, ("osum0", "osum1"))
-    event("end", ("x1",), waits=exchanged(1), cost=3.0, late=1, work=finish)
+                cost=0.7, late=1, work=functools.partial(project, p, dx, n == 0),
+            )
+        event(f"osum{p}", [f"p{p}3"], cost=0.2, late=1, work=functools.partial(out_sums, p))
+        exchange(1, p, [f"osum{p}"])
+        event(f"end{p}", (f"x1{p}",), waits=exchanged(1, p), cost=1.2, late=1, work=functools.partial(finish, p))
     run()
+    for copy in written:
+        copy.wait()
     for copy in sends:
         copy.wait_send()
 
@@ -522,16 +539,16 @@
             pltpu.VMEM((4, CAP, TCOL), bf),
             pltpu.VMEM((2, HALF, TCOL), bf),
             pltpu.VMEM((CAP, QKV), fl),
-            pltpu.VMEM((CAP, QW + 128), bf),
+            pltpu.VMEM((6, CAP, 128), bf),
             pltpu.VMEM((CAP, 128), bf),
             pltpu.VMEM((4, CAP, QW), bf),
             pltpu.VMEM((2, HALF, QW), bf),
             pltpu.VMEM((CAP, TCOL), fl),
             pltpu.VMEM((CAP, TCOL), bf),
-            pltpu.VMEM((2, 128, CAP), fl),
-            pltpu.VMEM((2, 3, 8, CAP), fl),
-            pltpu.VMEM((8, CAP), fl),
-            pltpu.VMEM((CAP, 128), fl),
+            pltpu.VMEM((2, 2, 128, HALF), fl),
+            pltpu.VMEM((2, 2, 3, 8, HALF), fl),
+            pltpu.VMEM((2, 8, HALF), fl),
+            pltpu.VMEM((2, HALF, 128), fl),
             pltpu.SemaphoreType.DMA((SEM_N,)),
             pltpu.SemaphoreType.DMA((SEM_N,)),
             pltpu.SemaphoreType.DMA((5,)),

time: 135 us -> 125 us (0.926)
  Pallas kernels: 124 us -> 114 us
    pallas_call x1, Pallas kernels: 124 us -> 114 us  [body(): pl.pallas_call(kernel, out_shape=jax.ShapeDtypeStruct((CAP, TCOL), bf), i...]
where the time goes in v3:
time: 125 us
  Pallas kernels  114 us (91%)
  local copies, waits for them, and re-layouts  6.42 us (5%)
  other arithmetic  4.04 us (3%)
    pallas_call x1, Pallas kernels, body(): pl.pallas_call(kernel, out_shape=jax.ShapeDtypeStruct((CAP, TCOL), bf), i...  114 us
    unnamed x1, local copies, waits for them, and re-layouts  2.94 us

profile of v3, /device:TPU:1, one launch (start us, length us, event | category | flops | bytes accessed | tf_op | source)
XLA Modules:
  0.0 124.8 jit_solution(12567645729115944006)
XLA Ops:
  0.7 0.7 pad_maximum_fusion.2
  1.4 0.6 broadcast_in_dim.12.gain_ref
  2.0 0.7 subtract_convert_fusion
  2.7 1.3 %broadcast_in_dim.13.ogain_ref = f32[1,1280]{1,0:T(1,128)} reshape(f32[1280]{0:T(1024)} %param.19) | data formatting | bytes 10240 | tf_op jit(solution)/shard_map/broadcast_in_dim | solution.py:569
  4.0 1.6 %broadcast_in_dim.14.start_ref = s32[768,1]{1,0:T(8,128)} reshape(s32[768]{0:T(1024)} %param.12) | data formatting | bytes 6144 | tf_op jit(solution)/shard_map/broadcast_in_dim | solution.py:567
  5.6 1.4 %fusion = (f32[768,64]{1,0:T(8,128)S(1)}, f32[768,64]{1,0:T(8,128)S(1)}, f32[768,64]{1,0:T(8,128)S(1)}) fusion(f32[64]{0:T(128)S(1)} %negate_power_fusion, f32[768]{0:T(1024)S(1)} %subtract_convert_fusion), kind=kLoop, calls=%fused_computation.4 | loop fusion | flops 98304 | bytes 593152 | tf_op jit(solution)/shard_map/neg | solution.py:525
  7.0 1.2 pad_maximum_fusion
  8.2 113.6 %shard_map.100 = bf16[768,1280]{1,0:T(8,128)(2,1)} custom-call(bf16[768,1280]{1,0:T(8,128)(2,1)} %tok_hbm.1, bf16[160,640]{1,0:T(8,128)(2,1)} %wq_hbm.1, bf16[160,128]{1,0:T(8,128)(2,1)} %wk_hbm.1, bf16[160,128]{1,0:T(8,128)(2,1)} %wv_hbm.1, bf16[160,640]{1,0:T(8,128)(2,1)} %bitcast.1, f32[768,128]{1,0:T(8,128)} %get-tuple-element.8.cos_ref, ...), custom_call_target="tpu_custom_call" | custom-call | tf_op jit(solution)/shard_map/pallas_call | solution.py:531
  121.8 2.9 %copy.14 = bf16[768,1280]{1,0:T(8,128)(2,1)} copy(bf16[768,1280]{1,0:T(8,128)(2,1)} %shard_map.100) | data formatting | bytes 3932160
  (1 shorter events, 0.0 us)

commit v4 on v3

--- a/solution.py
+++ b/solution.py
@@ -78,11 +78,10 @@
     wk_hbm,
     wv_hbm,
     wot_hbm,
-    cos_ref,
-    sin_ref,
-    start_ref,
-    gain_ref,
-    ogain_ref,
+    first_hbm,
+    qgain_hbm,
+    kgain_hbm,
+    ogain_hbm,
     live_ref,
     out_hbm,
     wbuf,
@@ -100,6 +99,13 @@
     sqr,
     krow,
     qcol,
+    cos_ref,
+    sin_ref,
+    start_ref,
+    first_v,
+    qgain_v,
+    kgain_v,
+    ogain_v,
     send_sem,
     recv_sem,
     local_sem,
@@ -170,6 +176,10 @@
         pltpu.make_async_copy(wk_hbm, wbuf.at[x, yl, z, :, pl.ds(QW, 128)], local_sem.at[1]),
         pltpu.make_async_copy(wv_hbm, wbuf.at[x, yl, z, :, pl.ds(QW + 128, 128)], local_sem.at[2]),
         pltpu.make_async_copy(tok_hbm, xall.at[t], local_sem.at[3]),
+        pltpu.make_async_copy(first_hbm, first_v, local_sem.at[5]),
+        pltpu.make_async_copy(qgain_hbm, qgain_v, local_sem.at[6]),
+        pltpu.make_async_copy(kgain_hbm, kgain_v, local_sem.at[7]),
+        pltpu.make_async_copy(ogain_hbm, ogain_v, local_sem.at[8]),
     ]
     for copy in local:
         copy.start()
@@ -366,11 +376,25 @@
         both = jnp.where(lane < 4, qs, ks)
         sqt[0, p] = both.T
 
+    def tables():
+        for copy in local[4:]:
+            copy.wait()
+        first = jnp.broadcast_to(first_v[...].reshape(1, CAP), (128, CAP)).astype(jnp.float32).T
+        wide = lax.broadcasted_iota(jnp.int32, (CAP, 128), 1)
+        local_row = lax.broadcasted_iota(jnp.int32, (CAP, 128), 0).astype(jnp.float32)
+        freqs = jnp.power(ROPE_BASE, -((wide % 64).astype(jnp.float32) * 2.0 / HEAD_DIM))
+        angle = (local_row - first) * freqs
+        sine = jnp.sin(angle)
+        cos_ref[...] = jnp.cos(angle)
+        sin_ref[...] = jnp.where(wide < 64, -sine, sine)
+        start_ref[...] = first.astype(jnp.int32)
+
     def rotate(p):
         rows = pl.ds(p * HALF, HALF)
+        gains = jnp.concatenate([qgain_v[...].reshape(1, QW), kgain_v[...].reshape(1, 128)], axis=1)
         for h in range(6):
             cols = pl.ds(h * 128, 128)
-            u = acc[rows, cols] * gain_ref[:, cols]
+            u = acc[rows, cols] * gains[:, h * 128 : (h + 1) * 128]
             r = u * cos_ref[rows] + pltpu.roll(u, 64, 1) * sin_ref[rows]
             rot[h, rows] = r.astype(jnp.bfloat16)
         vbuf[rows] = acc[rows, pl.ds(QW + 128, 128)].astype(jnp.bfloat16)
@@ -387,7 +411,7 @@
         rows = pl.ds(p * HALF + b * 128, 128)
         width = (b + 1) * 128
         seen = pl.ds(p * HALF, width)
-        first = start_ref[rows] - p * HALF
+        first = start_ref[rows, 0:1] - p * HALF
         col = lax.broadcasted_iota(jnp.int32, (128, width), 1)
         row = lax.broadcasted_iota(jnp.int32, (128, width), 0) + b * 128
         bias = jnp.where((col >= first) & (col <= row), 0.0, -1e30).astype(jnp.float32)
@@ -429,7 +453,7 @@
         sums_out = jnp.concatenate([total(1, p)] * 16, axis=0).T
         rows = pl.ds(p * HALF, HALF)
         scale = lax.rsqrt(sums_out[:, 0:1] / D + EPS)
-        r = xall[t, rows].astype(jnp.float32) + oacc[rows] * scale * ogain_ref[...]
+        r = xall[t, rows].astype(jnp.float32) + oacc[rows] * scale * ogain_v[...].reshape(1, TCOL)
         row = lax.broadcasted_iota(jnp.int32, (HALF, TCOL), 0) + p * HALF
         res[rows] = jnp.where(row < live_ref[0], r, 0.0).astype(jnp.bfloat16)
         written[p].start()
@@ -475,6 +499,7 @@
     event("swapped", ("swap", "tr5"), cost=0.1, work=swap_in)
     gather("o", obuf, SEM_O, 102.4, ["swapped"] + w_sends, ["swapped"], True)
     event("own", work=local[3].wait)
+    event("tables", ["to11"], cost=3.0, late=1, work=tables)
 
     for p in range(2):
         blocks = [(0, HALF)] if p == 0 else [(HALF, HALF // 2), (HALF + HALF // 2, HALF // 2)]
@@ -488,7 +513,7 @@
                 )
         event(f"sum{p}", [f"q{p}{m}3" for m in range(len(blocks))], cost=0.2, late=1, work=functools.partial(sums, p))
         exchange(0, p, [f"sum{p}"])
-        event(f"rot{p}", [f"x0{p}"], cost=0.4, late=1, work=functools.partial(rotate, p))
+        event(f"rot{p}", [f"x0{p}", "tables"], cost=0.4, late=1, work=functools.partial(rotate, p))
         event(f"scale{p}", [f"rot{p}"], waits=exchanged(0, p), cost=0.2, late=1, work=functools.partial(scales, p))
     half_a = ATT_N // 2
     for i in range(ATT_N):
@@ -516,23 +541,14 @@
 def body(
     tokens, live_rows, first_row, w_query, w_key, w_value, w_out, query_gain, key_gain, out_gain
 ):
-    half = HEAD_DIM // 2
-    freqs = jnp.power(ROPE_BASE, -(jnp.arange(half, dtype=jnp.float32) * 2.0 / HEAD_DIM))
-    positions = (jnp.arange(CAP, dtype=jnp.int32) - first_row).astype(jnp.float32)
-    angle = positions[:, None] * freqs[None, :]
-    cosine, sine = jnp.cos(angle), jnp.sin(angle)
-    cos = jnp.concatenate([cosine, cosine], axis=1)
-    sin = jnp.concatenate([-sine, sine], axis=1)
-    gains = jnp.concatenate([query_gain, key_gain])[None, :]
-    hbm = pl.BlockSpec(memory_space=pl.ANY)
-    vmem = pl.BlockSpec(memory_space=pltpu.VMEM)
+    hbm = pl.BlockSpec(memory_space=pltpu.HBM)
     smem = pl.BlockSpec(memory_space=pltpu.SMEM)
     bf, fl = jnp.bfloat16, jnp.float32
     return pl.pallas_call(
         kernel,
         out_shape=jax.ShapeDtypeStruct((CAP, TCOL), bf),
-        in_specs=[hbm] * 5 + [vmem] * 5 + [smem],
-        out_specs=hbm,
+        in_specs=[hbm] * 9 + [smem],
+        out_specs=pl.BlockSpec(memory_space=pl.ANY),
         scratch_shapes=[
             pltpu.VMEM((4, 2, 4, SHARD, QKV), bf),
             pltpu.VMEM((4, 2, 4, SHARD, QW), bf),
@@ -549,9 +565,16 @@
             pltpu.VMEM((2, 2, 3, 8, HALF), fl),
             pltpu.VMEM((2, 8, HALF), fl),
             pltpu.VMEM((2, HALF, 128), fl),
+            pltpu.VMEM((CAP, 128), fl),
+            pltpu.VMEM((CAP, 128), fl),
+            pltpu.VMEM((CAP, 128), jnp.int32),
+            pltpu.VMEM((CAP,), jnp.int32),
+            pltpu.VMEM((QW,), fl),
+            pltpu.VMEM((128,), fl),
+            pltpu.VMEM((TCOL,), fl),
             pltpu.SemaphoreType.DMA((SEM_N,)),
             pltpu.SemaphoreType.DMA((SEM_N,)),
-            pltpu.SemaphoreType.DMA((5,)),
+            pltpu.SemaphoreType.DMA((9,)),
         ],
         compiler_params=pltpu.CompilerParams(
             collective_id=0, has_side_effects=True, vmem_limit_bytes=60 * 1024 * 1024
@@ -562,11 +585,10 @@
         w_key,
         w_value,
         w_out.T,
-        cos,
-        sin,
-        first_row[:, None],
-        gains,
-        out_gain[None, :],
+        first_row,
+        query_gain,
+        key_gain,
+        out_gain,
         live_rows,
     )
 

time: 125 us -> 116 us (0.928)
  other arithmetic: 4.04 us -> 0 us
  local copies, waits for them, and re-layouts: 6.42 us -> 2.94 us
    broadcast_in_dim x3 -> x0, local copies, waits for them, and re-layouts: 3.48 us -> none  [the longest x1 1.6 us: body(): first_row[:, None]]
    concatenate x2 -> x0, other arithmetic: 1.9 us -> none  [the longest x1 1.19 us: body(): cos = jnp.concatenate([cosine, cosine], axis=1)]
    neg x1 -> x0, other arithmetic: 1.44 us -> none  [body(): sin = jnp.concatenate([-sine, sine], axis=1)]
where the time goes in v4:
time: 116 us
  Pallas kernels  113 us (97%)
  local copies, waits for them, and re-layouts  2.94 us (3%)
    pallas_call x1, Pallas kernels, body(): pl.pallas_call(kernel, out_shape=jax.ShapeDtypeStruct((CAP, TCOL), bf), i...  113 us
    unnamed x1, local copies, waits for them, and re-layouts  2.94 us

profile of v4, /device:TPU:1, one launch (start us, length us, event | category | flops | bytes accessed | tf_op | source)
XLA Modules:
  0.0 116.3 jit_solution(3255572107086479925)
XLA Ops:
  0.7 112.7 %shard_map.100 = bf16[768,1280]{1,0:T(8,128)(2,1)} custom-call(bf16[768,1280]{1,0:T(8,128)(2,1)} %tok_hbm.1, bf16[160,640]{1,0:T(8,128)(2,1)} %wq_hbm.1, bf16[160,128]{1,0:T(8,128)(2,1)} %wk_hbm.1, bf16[160,128]{1,0:T(8,128)(2,1)} %wv_hbm.1, bf16[160,640]{1,0:T(8,128)(2,1)} %bitcast.1, s32[768]{0:T(1024)} %first_hbm.1, f32[640]{0:T(1024)} %qgain_hbm.1, ...), custom_call_target="tpu_custom_call" | custom-call | tf_op jit(solution)/shard_map/pallas_call | solution.py:547
  113.3 2.9 %copy.13 = bf16[768,1280]{1,0:T(8,128)(2,1)} copy(bf16[768,1280]{1,0:T(8,128)(2,1)} %shard_map.100) | data formatting | bytes 3932160

commit v5 on v4

--- a/solution.py
+++ b/solution.py
@@ -22,7 +22,9 @@
 TCOL = 1280
 MESH = pl.DeviceIdType.MESH
 
-TOK_CHUNK = 64
+BLOCKS = 2
+
+TOK_CHUNK = 96
 TOK_N = CAP // TOK_CHUNK
 ATT_CHUNK = 128
 ATT_N = CAP // ATT_CHUNK
@@ -495,11 +497,11 @@
     gather("w", wbuf, SEM_W, 143.4, (), (), False)
     event("swap", ("w010", "w011"), sends=[(SEM_P, "far", 205, lambda idx: swap_out())])
     for i in range(TOK_N):
-        spread("t", xall, xstage, SEM_T, TOK_CHUNK, i, 163.8, ("wy0", "wy1", "w010", "w011"), tok_hbm)
-    event("swapped", ("swap", "tr5"), cost=0.1, work=swap_in)
-    gather("o", obuf, SEM_O, 102.4, ["swapped"] + w_sends, ["swapped"], True)
+        spread("t", xall, xstage, SEM_T, TOK_CHUNK, i, 245.8, ("wy0", "wy1", "w010", "w011"), tok_hbm)
+    event("swapped", ("swap", "tr3"), cost=0.1, work=swap_in)
+    gather("o", obuf, SEM_O, 102.4, ["swapped"] + w_sends, ["swapped", "tr7"], False)
     event("own", work=local[3].wait)
-    event("tables", ["to11"], cost=3.0, late=1, work=tables)
+    event("tables", ["to7"], cost=3.0, late=1, work=tables)
 
     for p in range(2):
         blocks = [(0, HALF)] if p == 0 else [(HALF, HALF // 2), (HALF + HALF // 2, HALF // 2)]
@@ -538,13 +540,17 @@
         copy.wait_send()
 
 
+def put_out(src, dst):
+    dst[...] = src[...]
+
+
 def body(
     tokens, live_rows, first_row, w_query, w_key, w_value, w_out, query_gain, key_gain, out_gain
 ):
     hbm = pl.BlockSpec(memory_space=pltpu.HBM)
     smem = pl.BlockSpec(memory_space=pltpu.SMEM)
     bf, fl = jnp.bfloat16, jnp.float32
-    return pl.pallas_call(
+    result = pl.pallas_call(
         kernel,
         out_shape=jax.ShapeDtypeStruct((CAP, TCOL), bf),
         in_specs=[hbm] * 9 + [smem],
@@ -591,6 +597,14 @@
         out_gain,
         live_rows,
     )
+    block = pl.BlockSpec((CAP // BLOCKS, TCOL), lambda i: (i, 0))
+    return pl.pallas_call(
+        put_out,
+        grid=(BLOCKS,),
+        out_shape=jax.ShapeDtypeStruct((CAP, TCOL), bf),
+        in_specs=[block],
+        out_specs=block,
+    )(result)
 
 
 def solution(mesh):

time: 116 us -> 115 us (level)
  local copies, waits for them, and re-layouts: 2.94 us -> 0 us
    unnamed x1 -> x0, local copies, waits for them, and re-layouts: 2.94 us -> none
    pallas_call x0 -> x1, Pallas kernels: none -> 2.54 us  [body(): pl.pallas_call(put_out, grid=(BLOCKS,), out_shape=jax.ShapeDtypeStruct((C...]
where the time goes in v5:
time: 115 us
  Pallas kernels  114 us (99%)
    pallas_call x1, Pallas kernels, body(): pl.pallas_call(kernel, out_shape=jax.ShapeDtypeStruct((CAP, TCOL), bf), i...  112 us
    pallas_call x1, Pallas kernels, body(): pl.pallas_call(put_out, grid=(BLOCKS,), out_shape=jax.ShapeDtypeStruct((C...  2.54 us

profile of v5, /device:TPU:1, one launch (start us, length us, event | category | flops | bytes accessed | tf_op | source)
XLA Modules:
  0.0 115.1 jit_solution(900244831759836063)
XLA Ops:
  0.7 111.9 %shard_map.100.src = bf16[768,1280]{1,0:T(8,128)(2,1)} custom-call(bf16[768,1280]{1,0:T(8,128)(2,1)} %tok_hbm.1, bf16[160,640]{1,0:T(8,128)(2,1)} %wq_hbm.1, bf16[160,128]{1,0:T(8,128)(2,1)} %wk_hbm.1, bf16[160,128]{1,0:T(8,128)(2,1)} %wv_hbm.1, bf16[160,640]{1,0:T(8,128)(2,1)} %bitcast.1, s32[768]{0:T(1024)} %first_hbm.1, f32[640]{0:T(1024)} %qgain_hbm.1, ...), custom_call_target="tpu_custom_call" | custom-call | tf_op jit(solution)/shard_map/pallas_call | solution.py:553
  112.5 2.5 %shard_map.101 = bf16[768,1280]{1,0:T(8,128)(2,1)} custom-call(bf16[768,1280]{1,0:T(8,128)(2,1)} %shard_map.100.src), custom_call_target="tpu_custom_call" | custom-call | tf_op jit(solution)/shard_map/pallas_call | solution.py:601

commit v6 on v5

--- a/solution.py
+++ b/solution.py
@@ -22,7 +22,7 @@
 TCOL = 1280
 MESH = pl.DeviceIdType.MESH
 
-BLOCKS = 2
+BLOCKS = 3
 
 TOK_CHUNK = 96
 TOK_N = CAP // TOK_CHUNK

time: 115 us -> 116 us (level)
  Pallas kernels: 114 us -> 116 us
where the time goes in v6:
time: 116 us
  Pallas kernels  116 us (100%)
    pallas_call x1, Pallas kernels, body(): pl.pallas_call(kernel, out_shape=jax.ShapeDtypeStruct((CAP, TCOL), bf), i...  112 us
    pallas_call x1, Pallas kernels, body(): pl.pallas_call(put_out, grid=(BLOCKS,), out_shape=jax.ShapeDtypeStruct((C...  3.62 us

profile of v6, /device:TPU:1, one launch (start us, length us, event | category | flops | bytes accessed | tf_op | source)
XLA Modules:
  0.0 116.2 jit_solution(7812141723212203906)
XLA Ops:
  0.7 111.9 %shard_map.100.src = bf16[768,1280]{1,0:T(8,128)(2,1)} custom-call(bf16[768,1280]{1,0:T(8,128)(2,1)} %tok_hbm.1, bf16[160,640]{1,0:T(8,128)(2,1)} %wq_hbm.1, bf16[160,128]{1,0:T(8,128)(2,1)} %wk_hbm.1, bf16[160,128]{1,0:T(8,128)(2,1)} %wv_hbm.1, bf16[160,640]{1,0:T(8,128)(2,1)} %bitcast.1, s32[768]{0:T(1024)} %first_hbm.1, f32[640]{0:T(1024)} %qgain_hbm.1, ...), custom_call_target="tpu_custom_call" | custom-call | tf_op jit(solution)/shard_map/pallas_call | solution.py:553
  112.5 3.6 %shard_map.101 = bf16[768,1280]{1,0:T(8,128)(2,1)} custom-call(bf16[768,1280]{1,0:T(8,128)(2,1)} %shard_map.100.src), custom_call_target="tpu_custom_call" | custom-call | tf_op jit(solution)/shard_map/pallas_call | solution.py:601
